TPU v7x, 128 devices: a whole 4x4x4 slice. The times are simulated.
128 devices in a mesh: row: 16 (over z_lo, y, core), feat: 8 (over z_hi, x).
Axes of the slice: x: 4, y: 4, z: 4 (z_hi: 2, z_lo: 2; z = z_hi * 2 + z_lo), core: 2. Of those that a mesh axis runs over, the one named last changes fastest.
Arguments:
- features: bfloat16 [16384, 2048], P('row', 'feat'), may hold values from -6 to 6
- cut_points: float32 [2048, 256], P('feat'), as said below
- grad: float32 [16384], P('row'), may hold values from -1 to 1
- hess: float32 [16384], P('row'), may hold values from 0.05 to 0.25
- node_ids: int32 [16384], P('row'), may hold values from 0 to 31
Outputs:
- feature_gain: float32 [2048, 32], P(('feat', 'row'))
- node_best: float32 [32], replicated
Inputs may be any that keep to these rules, and one draw needn't show every extreme that they name: Each row of cut_points rises strictly.
All inputs are finite; a program needn't handle non-finite values.
Results may differ from a plain program's by a relative error of at most 0.0065.
Values may be sent and summed in bfloat16 or wider, within the bound.
No kernel may reach another device: no remote copies, remote signals or barrier semaphores. Data moves between devices by JAX's collectives and lax.ppermute only.
A program may use at most 128 MiB of HBM per device.

v0:
```python
import math

import jax
import jax.numpy as jnp
from jax import lax
from jax.sharding import PartitionSpec as P

NODES = 32


PENALTY = 1.0


def row_weights(grad, hess, node_ids):
    member = (node_ids[:, None] == jnp.arange(NODES, dtype=jnp.int32)[None, :]).astype(jnp.float32)
    return jnp.concatenate([grad[:, None] * member, hess[:, None] * member], axis=1).astype(
        jnp.bfloat16
    )


def split_gains(histogram, totals):
    half = totals.shape[0] // 2
    grad_left = jnp.cumsum(histogram[:, :, :half], axis=1)
    hess_left = jnp.cumsum(histogram[:, :, half:], axis=1)
    grad_total = totals[:half]
    hess_total = totals[half:]
    split_gain = jnp.square(grad_left) / (hess_left + PENALTY)
    split_gain = split_gain + jnp.square(grad_total - grad_left) / (
        hess_total - hess_left + PENALTY
    )
    split_gain = split_gain - jnp.square(grad_total) / (hess_total + PENALTY)
    return jnp.max(split_gain, axis=1)


def onehot_hist(values, edges, weights):
    row_count, feat_count = values.shape
    bin_count = edges.shape[1]
    width = weights.shape[1]
    row_block = math.gcd(row_count, 2048)
    feat_block = math.gcd(feat_count, 16)
    upper_edge = jnp.concatenate(
        [edges[:, 1:], jnp.full((feat_count, 1), jnp.inf, jnp.float32)], axis=1
    )
    lower_blocks = edges.reshape(feat_count // feat_block, feat_block, bin_count)
    upper_blocks = upper_edge.reshape(feat_count // feat_block, feat_block, bin_count)
    value_blocks = values.reshape(
        row_count // row_block, row_block, feat_count // feat_block, feat_block
    )
    value_blocks = value_blocks.transpose(2, 0, 1, 3)
    weight_blocks = weights.reshape(row_count // row_block, row_block, width)

    def feature_block(triple):
        block_values, lower_edge, upper_bound = triple

        def accumulate(running, pair):
            piece_values, piece_weights = pair
            valued = piece_values.astype(jnp.float32)[:, :, None]
            indicator = ((valued >= lower_edge[None]) & (valued < upper_bound[None])).astype(
                jnp.bfloat16
            )
            product = jnp.einsum(
                "rfb,rk->fbk", indicator, piece_weights, preferred_element_type=jnp.float32
            )
            return (running + product, None)

        start_total = jnp.zeros((feat_block, bin_count, width), jnp.float32)
        running, _ = lax.scan(accumulate, start_total, (block_values, weight_blocks))
        return running

    blocks = lax.map(feature_block, (value_blocks, lower_blocks, upper_blocks))
    return blocks.reshape(feat_count, bin_count, width)


def on_device(features, cut_points, grad, hess, node_ids):
    weights = row_weights(grad, hess, node_ids)
    totals = lax.psum(jnp.sum(weights.astype(jnp.float32), axis=0), "row")
    row_parts = lax.axis_size("row")
    scored = cut_points.shape[0] // row_parts
    offset = lax.axis_index("row") * scored
    summed = lax.psum(onehot_hist(features, cut_points, weights), "row")
    owned_hist = lax.dynamic_slice_in_dim(summed, offset, scored, 0)
    feature_gain = split_gains(owned_hist, totals)
    node_best = lax.pmax(jnp.max(feature_gain, axis=0), ("row", "feat"))
    return (feature_gain, node_best)


def solution(mesh):
    placed = (P("row", "feat"), P("feat", None), P("row"), P("row"), P("row"))
    return jax.shard_map(
        on_device,
        mesh=mesh,
        in_specs=placed,
        out_specs=(P(("feat", "row"), None), P()),
        check_vma=False,
    )
```

profile of v0, /device:TPU:1, one launch (start us, length us, event | category | flops | bytes accessed | tf_op | source)
XLA Modules:
  0.0 412.0 jit_solution(5966503884586847669)
XLA Ops:
  7.2 0.0 all-reduce.3.cloned.1.call-start
  7.2 1.2 copy.8
  8.5 1.1 slice.27
  9.6 0.7 select_convert_fusion.1
  10.4 108.7 %while.10 = (s32[]{:T(128)}, f32[16,16,256,64]{2,3,1,0:T(8,128)}, bf16[16,1,1024,16]{2,3,1,0:T(8,128)(2,1)S(1)}, f32[16,16,256]{2,1,0:T(8,128)}, f32[16,16,256]{...) while((s32[]{:T(128)}, f32[16,16,256,64]{2,3,1,0:T(8,128)}, ...), condition=%wide.region_1.0_spmd, body=%wide.region_0.0_spmd.sunk | while | flops 549470208 | bytes 1441889 | solution.py:70
  10.4 0.7 dynamic-slice_bitcast_fusion.5
  11.1 6.1 %fusion.24 = f32[16,16,256,64]{2,3,1,0:T(8,128)} fusion(f32[16,16,256,64]{2,3,1,0:T(8,128)} %get-tuple-element.131, s32[]{:T(128)S(6)} %copy.28, f32[16,256]{1,0:T(8,128)S(1)} %get-tuple-element.121, f32[16,256]{1,0:T(8,128)S(1)} %get-tuple-element.122, f32[1024,16]{0,1:T(8,128)S(1)} %bitcast_convert_fusion.2, ...), kind=kOutput, calls=%fused_computation.6.clone.1 | convolution fusion | flops 549453824 | bytes 1277956 | tf_op jit(solution)/shard_map/while/body/eval_jaxpr/while/body/eval_jaxpr/rfb,rk->fbk/dot_general | solution.py:61
  17.2 0.7 dynamic-slice_bitcast_fusion.5
  17.9 6.1 %fusion.24 = f32[16,16,256,64]{2,3,1,0:T(8,128)} fusion(f32[16,16,256,64]{2,3,1,0:T(8,128)} %get-tuple-element.131, s32[]{:T(128)S(6)} %copy.28, f32[16,256]{1,0:T(8,128)S(1)} %get-tuple-element.121, f32[16,256]{1,0:T(8,128)S(1)} %get-tuple-element.122, f32[1024,16]{0,1:T(8,128)S(1)} %bitcast_convert_fusion.2, ...), kind=kOutput, calls=%fused_computation.6.clone.1 | convolution fusion | flops 549453824 | bytes 1277956 | tf_op jit(solution)/shard_map/while/body/eval_jaxpr/while/body/eval_jaxpr/rfb,rk->fbk/dot_general | solution.py:61
  24.0 0.7 dynamic-slice_bitcast_fusion.5
  24.7 6.1 %fusion.24 = f32[16,16,256,64]{2,3,1,0:T(8,128)} fusion(f32[16,16,256,64]{2,3,1,0:T(8,128)} %get-tuple-element.131, s32[]{:T(128)S(6)} %copy.28, f32[16,256]{1,0:T(8,128)S(1)} %get-tuple-element.121, f32[16,256]{1,0:T(8,128)S(1)} %get-tuple-element.122, f32[1024,16]{0,1:T(8,128)S(1)} %bitcast_convert_fusion.2, ...), kind=kOutput, calls=%fused_computation.6.clone.1 | convolution fusion | flops 549453824 | bytes 1277956 | tf_op jit(solution)/shard_map/while/body/eval_jaxpr/while/body/eval_jaxpr/rfb,rk->fbk/dot_general | solution.py:61
  30.8 0.7 dynamic-slice_bitcast_fusion.5
  31.5 6.1 %fusion.24 = f32[16,16,256,64]{2,3,1,0:T(8,128)} fusion(f32[16,16,256,64]{2,3,1,0:T(8,128)} %get-tuple-element.131, s32[]{:T(128)S(6)} %copy.28, f32[16,256]{1,0:T(8,128)S(1)} %get-tuple-element.121, f32[16,256]{1,0:T(8,128)S(1)} %get-tuple-element.122, f32[1024,16]{0,1:T(8,128)S(1)} %bitcast_convert_fusion.2, ...), kind=kOutput, calls=%fused_computation.6.clone.1 | convolution fusion | flops 549453824 | bytes 1277956 | tf_op jit(solution)/shard_map/while/body/eval_jaxpr/while/body/eval_jaxpr/rfb,rk->fbk/dot_general | solution.py:61
  37.6 0.7 dynamic-slice_bitcast_fusion.5
  38.3 6.1 %fusion.24 = f32[16,16,256,64]{2,3,1,0:T(8,128)} fusion(f32[16,16,256,64]{2,3,1,0:T(8,128)} %get-tuple-element.131, s32[]{:T(128)S(6)} %copy.28, f32[16,256]{1,0:T(8,128)S(1)} %get-tuple-element.121, f32[16,256]{1,0:T(8,128)S(1)} %get-tuple-element.122, f32[1024,16]{0,1:T(8,128)S(1)} %bitcast_convert_fusion.2, ...), kind=kOutput, calls=%fused_computation.6.clone.1 | convolution fusion | flops 549453824 | bytes 1277956 | tf_op jit(solution)/shard_map/while/body/eval_jaxpr/while/body/eval_jaxpr/rfb,rk->fbk/dot_general | solution.py:61
  44.3 0.7 dynamic-slice_bitcast_fusion.5
  45.1 6.1 %fusion.24 = f32[16,16,256,64]{2,3,1,0:T(8,128)} fusion(f32[16,16,256,64]{2,3,1,0:T(8,128)} %get-tuple-element.131, s32[]{:T(128)S(6)} %copy.28, f32[16,256]{1,0:T(8,128)S(1)} %get-tuple-element.121, f32[16,256]{1,0:T(8,128)S(1)} %get-tuple-element.122, f32[1024,16]{0,1:T(8,128)S(1)} %bitcast_convert_fusion.2, ...), kind=kOutput, calls=%fused_computation.6.clone.1 | convolution fusion | flops 549453824 | bytes 1277956 | tf_op jit(solution)/shard_map/while/body/eval_jaxpr/while/body/eval_jaxpr/rfb,rk->fbk/dot_general | solution.py:61
  51.1 0.7 dynamic-slice_bitcast_fusion.5
  51.9 6.1 %fusion.24 = f32[16,16,256,64]{2,3,1,0:T(8,128)} fusion(f32[16,16,256,64]{2,3,1,0:T(8,128)} %get-tuple-element.131, s32[]{:T(128)S(6)} %copy.28, f32[16,256]{1,0:T(8,128)S(1)} %get-tuple-element.121, f32[16,256]{1,0:T(8,128)S(1)} %get-tuple-element.122, f32[1024,16]{0,1:T(8,128)S(1)} %bitcast_convert_fusion.2, ...), kind=kOutput, calls=%fused_computation.6.clone.1 | convolution fusion | flops 549453824 | bytes 1277956 | tf_op jit(solution)/shard_map/while/body/eval_jaxpr/while/body/eval_jaxpr/rfb,rk->fbk/dot_general | solution.py:61
  57.9 0.7 dynamic-slice_bitcast_fusion.5
  58.7 6.1 %fusion.24 = f32[16,16,256,64]{2,3,1,0:T(8,128)} fusion(f32[16,16,256,64]{2,3,1,0:T(8,128)} %get-tuple-element.131, s32[]{:T(128)S(6)} %copy.28, f32[16,256]{1,0:T(8,128)S(1)} %get-tuple-element.121, f32[16,256]{1,0:T(8,128)S(1)} %get-tuple-element.122, f32[1024,16]{0,1:T(8,128)S(1)} %bitcast_convert_fusion.2, ...), kind=kOutput, calls=%fused_computation.6.clone.1 | convolution fusion | flops 549453824 | bytes 1277956 | tf_op jit(solution)/shard_map/while/body/eval_jaxpr/while/body/eval_jaxpr/rfb,rk->fbk/dot_general | solution.py:61
  64.7 0.7 dynamic-slice_bitcast_fusion.5
  65.5 6.1 %fusion.24 = f32[16,16,256,64]{2,3,1,0:T(8,128)} fusion(f32[16,16,256,64]{2,3,1,0:T(8,128)} %get-tuple-element.131, s32[]{:T(128)S(6)} %copy.28, f32[16,256]{1,0:T(8,128)S(1)} %get-tuple-element.121, f32[16,256]{1,0:T(8,128)S(1)} %get-tuple-element.122, f32[1024,16]{0,1:T(8,128)S(1)} %bitcast_convert_fusion.2, ...), kind=kOutput, calls=%fused_computation.6.clone.1 | convolution fusion | flops 549453824 | bytes 1277956 | tf_op jit(solution)/shard_map/while/body/eval_jaxpr/while/body/eval_jaxpr/rfb,rk->fbk/dot_general | solution.py:61
  71.5 0.7 dynamic-slice_bitcast_fusion.5
  72.3 6.1 %fusion.24 = f32[16,16,256,64]{2,3,1,0:T(8,128)} fusion(f32[16,16,256,64]{2,3,1,0:T(8,128)} %get-tuple-element.131, s32[]{:T(128)S(6)} %copy.28, f32[16,256]{1,0:T(8,128)S(1)} %get-tuple-element.121, f32[16,256]{1,0:T(8,128)S(1)} %get-tuple-element.122, f32[1024,16]{0,1:T(8,128)S(1)} %bitcast_convert_fusion.2, ...), kind=kOutput, calls=%fused_computation.6.clone.1 | convolution fusion | flops 549453824 | bytes 1277956 | tf_op jit(solution)/shard_map/while/body/eval_jaxpr/while/body/eval_jaxpr/rfb,rk->fbk/dot_general | solution.py:61
  78.3 0.7 dynamic-slice_bitcast_fusion.5
  79.1 6.1 %fusion.24 = f32[16,16,256,64]{2,3,1,0:T(8,128)} fusion(f32[16,16,256,64]{2,3,1,0:T(8,128)} %get-tuple-element.131, s32[]{:T(128)S(6)} %copy.28, f32[16,256]{1,0:T(8,128)S(1)} %get-tuple-element.121, f32[16,256]{1,0:T(8,128)S(1)} %get-tuple-element.122, f32[1024,16]{0,1:T(8,128)S(1)} %bitcast_convert_fusion.2, ...), kind=kOutput, calls=%fused_computation.6.clone.1 | convolution fusion | flops 549453824 | bytes 1277956 | tf_op jit(solution)/shard_map/while/body/eval_jaxpr/while/body/eval_jaxpr/rfb,rk->fbk/dot_general | solution.py:61
  85.1 0.7 dynamic-slice_bitcast_fusion.5
  85.8 6.1 %fusion.24 = f32[16,16,256,64]{2,3,1,0:T(8,128)} fusion(f32[16,16,256,64]{2,3,1,0:T(8,128)} %get-tuple-element.131, s32[]{:T(128)S(6)} %copy.28, f32[16,256]{1,0:T(8,128)S(1)} %get-tuple-element.121, f32[16,256]{1,0:T(8,128)S(1)} %get-tuple-element.122, f32[1024,16]{0,1:T(8,128)S(1)} %bitcast_convert_fusion.2, ...), kind=kOutput, calls=%fused_computation.6.clone.1 | convolution fusion | flops 549453824 | bytes 1277956 | tf_op jit(solution)/shard_map/while/body/eval_jaxpr/while/body/eval_jaxpr/rfb,rk->fbk/dot_general | solution.py:61
  91.9 0.7 dynamic-slice_bitcast_fusion.5
  92.6 6.1 %fusion.24 = f32[16,16,256,64]{2,3,1,0:T(8,128)} fusion(f32[16,16,256,64]{2,3,1,0:T(8,128)} %get-tuple-element.131, s32[]{:T(128)S(6)} %copy.28, f32[16,256]{1,0:T(8,128)S(1)} %get-tuple-element.121, f32[16,256]{1,0:T(8,128)S(1)} %get-tuple-element.122, f32[1024,16]{0,1:T(8,128)S(1)} %bitcast_convert_fusion.2, ...), kind=kOutput, calls=%fused_computation.6.clone.1 | convolution fusion | flops 549453824 | bytes 1277956 | tf_op jit(solution)/shard_map/while/body/eval_jaxpr/while/body/eval_jaxpr/rfb,rk->fbk/dot_general | solution.py:61
  98.7 0.7 dynamic-slice_bitcast_fusion.5
  99.4 6.1 %fusion.24 = f32[16,16,256,64]{2,3,1,0:T(8,128)} fusion(f32[16,16,256,64]{2,3,1,0:T(8,128)} %get-tuple-element.131, s32[]{:T(128)S(6)} %copy.28, f32[16,256]{1,0:T(8,128)S(1)} %get-tuple-element.121, f32[16,256]{1,0:T(8,128)S(1)} %get-tuple-element.122, f32[1024,16]{0,1:T(8,128)S(1)} %bitcast_convert_fusion.2, ...), kind=kOutput, calls=%fused_computation.6.clone.1 | convolution fusion | flops 549453824 | bytes 1277956 | tf_op jit(solution)/shard_map/while/body/eval_jaxpr/while/body/eval_jaxpr/rfb,rk->fbk/dot_general | solution.py:61
  105.5 0.7 dynamic-slice_bitcast_fusion.5
  106.2 6.1 %fusion.24 = f32[16,16,256,64]{2,3,1,0:T(8,128)} fusion(f32[16,16,256,64]{2,3,1,0:T(8,128)} %get-tuple-element.131, s32[]{:T(128)S(6)} %copy.28, f32[16,256]{1,0:T(8,128)S(1)} %get-tuple-element.121, f32[16,256]{1,0:T(8,128)S(1)} %get-tuple-element.122, f32[1024,16]{0,1:T(8,128)S(1)} %bitcast_convert_fusion.2, ...), kind=kOutput, calls=%fused_computation.6.clone.1 | convolution fusion | flops 549453824 | bytes 1277956 | tf_op jit(solution)/shard_map/while/body/eval_jaxpr/while/body/eval_jaxpr/rfb,rk->fbk/dot_general | solution.py:61
  112.3 0.7 dynamic-slice_bitcast_fusion.5
  113.0 6.1 %fusion.24 = f32[16,16,256,64]{2,3,1,0:T(8,128)} fusion(f32[16,16,256,64]{2,3,1,0:T(8,128)} %get-tuple-element.131, s32[]{:T(128)S(6)} %copy.28, f32[16,256]{1,0:T(8,128)S(1)} %get-tuple-element.121, f32[16,256]{1,0:T(8,128)S(1)} %get-tuple-element.122, f32[1024,16]{0,1:T(8,128)S(1)} %bitcast_convert_fusion.2, ...), kind=kOutput, calls=%fused_computation.6.clone.1 | convolution fusion | flops 549453824 | bytes 1277956 | tf_op jit(solution)/shard_map/while/body/eval_jaxpr/while/body/eval_jaxpr/rfb,rk->fbk/dot_general | solution.py:61
  119.1 0.0 all-reduce.3.cloned.1.call-update
  119.1 0.1 convert_reduce_fusion
  119.2 28.8 %psum.15 = f32[64]{0:T(128)S(1)} all-reduce(f32[64]{0:T(128)S(1)} %convert_reduce_fusion), channel_id=1, replica_groups=mesh['row'=16,'feat'=8] {'row'}, use_global_device_ids=true, to_apply=%region_8.9 | all-reduce | flops 64 | bytes 512 | tf_op jit(solution)/shard_map/psum | solution.py:76
  148.1 0.1 fusion.20
  148.1 169.0 %all-reduce.3.cloned.1.call-done = f32[256,256,64]{1,2,0:T(8,128)} async-done(((f32[256,256,64]{1,2,0:T(8,128)}), f32[256,256,64]{1,2,0:T(8,128)}) %all-reduce.3.cloned.1.call-update) | async-done | bytes 16777232 | tf_op jit(solution)/shard_map/psum | solution.py:80
  317.1 1.3 dynamic-slice_bitcast_fusion.3
  318.4 0.1 copy_bitcast_fusion
  318.5 9.2 %reduce-window.14 = f32[16,32,2,128]{3,1,2,0:T(8,128)S(1)} reduce-window(f32[16,32,2,128]{3,1,2,0:T(8,128)S(1)} %get-tuple-element.81, f32[]{:T(128)} %constant.24.clone.1), window={size=1x1x1x128 pad=0_0x0_0x0_0x127_0}, to_apply=%region_3.4 | reduce-window | flops 16646144 | bytes 1048580 | tf_op jit(solution)/shard_map/reduce-window
  327.8 0.2 slice.36
  328.0 0.3 copy.10
  328.2 0.1 fusion.15
  328.3 9.2 %reduce-window.16 = f32[16,32,2,128]{3,1,2,0:T(8,128)S(1)} reduce-window(f32[16,32,2,128]{3,1,2,0:T(8,128)S(1)} %get-tuple-element.80, f32[]{:T(128)} %constant.24.clone.1), window={size=1x1x1x128 pad=0_0x0_0x0_0x127_0}, to_apply=%region_5.6 | reduce-window | flops 16646144 | bytes 1048580 | tf_op jit(solution)/shard_map/reduce-window.2
  337.6 0.2 slice.38
  337.8 0.3 copy.14
  338.0 0.1 fusion.13
  338.1 1.1 fusion.19
  339.2 65.9 %pmax.7 = f32[32]{0:T(128)} all-reduce(f32[32]{0:T(128)S(1)} %get-tuple-element.53), channel_id=1, replica_groups=mesh['row'=16,'feat'=8] {'row','feat'}, use_global_device_ids=true, to_apply=%region_11.12 | all-reduce | flops 32 | bytes 256 | tf_op jit(solution)/shard_map/pmax | solution.py:83
  (23 shorter events, 0.2 us)
Async XLA Ops:
  7.2 309.9 %all-reduce.3.cloned.1.call-start = ((), (), s32[]{:S(2)}) async-start(), calls=%async_computation | async-start | bytes 33554432 | tf_op jit(solution)/shard_map/psum | solution.py:80
Sparse Core Ops, SparseCore 0:
  119.2 197.8 all-reduce.2
where the time goes:
time: 414 us; the launch traced here: 412 us
  waiting for transfers between devices  169 us (41%)
  matrix products  97 us (23%)
  blocking collectives  94.8 us (23%)
  other arithmetic  20.8 us (5%)
  local copies, waits for them, and re-layouts  16.2 us (4%)
  between operations  14.1 us (3%)
    psum x1, waiting for transfers between devices, on_device(): summed = lax.psum(onehot_hist(features, cut_points, weights), 'row')  169 us
    dot_general x16, matrix products, accumulate(): jnp.einsum('rfb,rk->fbk', indicator, piece_weights, preferred_element_typ...  97 us
    pmax x1, blocking collectives, on_device(): node_best = lax.pmax(jnp.max(feature_gain, axis=0), ('row', 'feat'))  65.9 us
    psum x1, blocking collectives, on_device(): totals = lax.psum(jnp.sum(weights.astype(jnp.float32), axis=0), 'row')  28.8 us
    another operation x5, other arithmetic  19.3 us
    lt x16, local copies, waits for them, and re-layouts, accumulate(): valued < upper_bound[None]  11.5 us
  transfers between devices with their start and end apart: 1, of which 1 were waited for; matrix products, arithmetic and copies ran while one was open for 0% of the time, Pallas kernels for 0%

commit v1 on v0

v1 whole, which is shorter than its diff:
```python
import functools

import jax
import jax.numpy as jnp
from jax import lax
from jax.experimental import pallas as pl
from jax.experimental.pallas import tpu as pltpu
from jax.sharding import PartitionSpec as P

NODES = 32
PENALTY = 1.0
SWAP = False


def round_up_bf16(edge):
    near = edge.astype(jnp.bfloat16).astype(jnp.float32)
    above = (near + jnp.abs(near) * (0.6 / 128)).astype(jnp.bfloat16).astype(jnp.float32)
    return jnp.where(near < edge, above, near)


def gain_kernel(rows_ref, edge_ref, gain_ref, weight_ref, edge_wide_ref, left_ref):
    groups, _, group_rows = rows_ref.shape
    feats, bins, _ = edge_wide_ref.shape

    for f in range(feats):
        edge_wide_ref[f] = jnp.broadcast_to(
            round_up_bf16(edge_ref[:, f : f + 1]), (bins, 128)
        ).astype(jnp.bfloat16)

    node_column = lax.broadcasted_iota(jnp.int32, (NODES, group_rows), 0).astype(jnp.float32)
    totals = jnp.zeros((2 * NODES, 128), jnp.float32)
    for s in range(groups):
        side = rows_ref[s, feats : feats + 3].astype(jnp.float32)
        member = node_column == side[2:3]
        weights = jnp.concatenate(
            [jnp.where(member, side[0:1], 0.0), jnp.where(member, side[1:2], 0.0)], axis=0
        )
        weight_ref[s] = weights.astype(jnp.bfloat16)

    def one_feature(f):
        edges = jnp.concatenate([edge_wide_ref[f]] * (group_rows // 128), axis=1)
        left_ref[...] = jnp.zeros_like(left_ref)

        @pl.loop(0, groups)
        def _(s):
            value = rows_ref[s, pl.ds(f, 1)]
            below = jnp.where(
                jnp.broadcast_to(value, edges.shape) < edges,
                jnp.bfloat16(1), jnp.bfloat16(0),
            )
            if SWAP:
                left_ref[...] += lax.dot_general(
                    weight_ref[s], below, (((1,), (1,)), ((), ())),
                    preferred_element_type=jnp.float32,
                )
            else:
                left_ref[...] += lax.dot_general(
                    below, weight_ref[s], (((1,), (1,)), ((), ())),
                    preferred_element_type=jnp.float32,
                )
        return left_ref[...]

    ones = jnp.ones((8, group_rows), jnp.bfloat16)
    total = jnp.zeros((8, 2 * NODES), jnp.float32)
    for s in range(groups):
        total = total + lax.dot_general(
            ones, weight_ref[s], (((1,), (1,)), ((), ())), preferred_element_type=jnp.float32
        )
    total = total[0:1]
    grad_total = total[:, :NODES]
    hess_total = total[:, NODES:]
    for f in range(feats):
        below = one_feature(f)
        if SWAP:
            below = below.T
        first = lax.broadcasted_iota(jnp.int32, below.shape, 0) == 0
        left = jnp.where(first, jnp.broadcast_to(total, below.shape), below) - below[0:1]
        grad_left = left[:, :NODES]
        hess_left = left[:, NODES:]
        split = jnp.square(grad_left) / (hess_left + PENALTY)
        split = split + jnp.square(grad_total - grad_left) / (hess_total - hess_left + PENALTY)
        split = split - jnp.square(grad_total) / (hess_total + PENALTY)
        gain_ref[f : f + 1] = jnp.max(split, axis=0, keepdims=True)


def on_device(features, cut_points, grad, hess, node_ids):
    parts = lax.axis_size("row")
    rows, feats = features.shape
    own = feats // parts
    bins = cut_points.shape[1]
    side = jnp.stack(
        [grad.astype(jnp.bfloat16), hess.astype(jnp.bfloat16), node_ids.astype(jnp.bfloat16)]
    )
    sent = jnp.concatenate(
        [features.T.reshape(parts, own, rows), jnp.broadcast_to(side[None], (parts, 3, rows))],
        axis=1,
    )
    gathered = lax.all_to_all(sent, "row", 0, 0)
    edges = lax.dynamic_slice_in_dim(cut_points, lax.axis_index("row") * own, own, 0).T
    feature_gain = pl.pallas_call(
        gain_kernel,
        out_shape=jax.ShapeDtypeStruct((own, NODES), jnp.float32),
        in_specs=[pl.BlockSpec(memory_space=pltpu.VMEM)] * 2,
        out_specs=pl.BlockSpec(memory_space=pltpu.VMEM),
        scratch_shapes=[
            pltpu.VMEM((parts, 2 * NODES, rows), jnp.bfloat16),
            pltpu.VMEM((own, bins, 128), jnp.bfloat16),
            pltpu.VMEM((2 * NODES, bins) if SWAP else (bins, 2 * NODES), jnp.float32),
        ],
        compiler_params=pltpu.CompilerParams(vmem_limit_bytes=40 << 20),
    )(gathered, edges)
    node_best = lax.pmax(jnp.max(feature_gain, axis=0), ("row", "feat"))
    return (feature_gain, node_best)


def solution(mesh):
    placed = (P("row", "feat"), P("feat", None), P("row"), P("row"), P("row"))
    return jax.shard_map(
        on_device,
        mesh=mesh,
        in_specs=placed,
        out_specs=(P(("feat", "row"), None), P()),
        check_vma=False,
    )
```

time: 414 us -> 169 us (0.41)
  waiting for transfers between devices: 169 us -> 12.9 us
  matrix products: 97 us -> 0 us
  Pallas kernels: 0 us -> 77.4 us
  blocking collectives: 94.8 us -> 65.1 us
  other arithmetic: 20.8 us -> 3.84 us
  local copies, waits for them, and re-layouts: 16.2 us -> 1.42 us
  between operations: 14.1 us -> 0.68 us
  starting transfers between devices: 0.04 us -> 7.34 us
    psum x1 -> x0, waiting for transfers between devices: 169 us -> none  [on_device(): summed = lax.psum(onehot_hist(features, cut_points, weights), 'row')]
    dot_general x16 -> x0, matrix products: 97 us -> none  [accumulate(): jnp.einsum('rfb,rk->fbk', indicator, piece_weights, preferred_element_typ...]
    pallas_call x0 -> x1, Pallas kernels: none -> 77.4 us  [on_device(): pl.pallas_call(gain_kernel, out_shape=jax.ShapeDtypeStruct((own, NODES),...]
    psum x1 -> x0, blocking collectives: 28.8 us -> none  [on_device(): totals = lax.psum(jnp.sum(weights.astype(jnp.float32), axis=0), 'row')]
    another operation x5 -> x1, other arithmetic: 19.3 us -> 0.02 us  [on_device(): jnp.stack([grad.astype(jnp.bfloat16), hess.astype(jnp.bfloat16), node_ids...]
    all_to_all x0 -> x1, waiting for transfers between devices: none -> 12.9 us  [on_device(): gathered = lax.all_to_all(sent, 'row', 0, 0)]
    lt x16 -> x0, local copies, waits for them, and re-layouts: 11.5 us -> none  [accumulate(): valued < upper_bound[None]]
    all_to_all x0 -> x1, starting transfers between devices: none -> 7.34 us  [on_device(): gathered = lax.all_to_all(sent, 'row', 0, 0)]
where the time goes in v1:
time: 169 us
  Pallas kernels  77.4 us (46%)
  blocking collectives  65.1 us (39%)
  waiting for transfers between devices  12.9 us (8%)
  starting transfers between devices  7.34 us (4%)
  other arithmetic  3.84 us (2%)
    pallas_call x1, Pallas kernels, on_device(): pl.pallas_call(gain_kernel, out_shape=jax.ShapeDtypeStruct((own, NODES),...  77.4 us
    pmax x1, blocking collectives, on_device(): node_best = lax.pmax(jnp.max(feature_gain, axis=0), ('row', 'feat'))  65.1 us
    all_to_all x1, waiting for transfers between devices, on_device(): gathered = lax.all_to_all(sent, 'row', 0, 0)  12.9 us
    all_to_all x1, starting transfers between devices, on_device(): gathered = lax.all_to_all(sent, 'row', 0, 0)  7.34 us
  transfers between devices with their start and end apart: 1, of which 1 were waited for; matrix products, arithmetic and copies ran while one was open for 0% of the time, Pallas kernels for 0%

profile of v1, /device:TPU:1, one launch (start us, length us, event | category | flops | bytes accessed | tf_op | source)
XLA Modules:
  0.0 168.7 jit_solution(13650751803497703946)
XLA Ops:
  0.6 0.0 copy-start
  0.6 0.7 convert_element_type.11
  1.4 0.7 convert_element_type.10
  2.1 0.7 convert_element_type.9
  2.8 1.2 copy.7
  4.1 1.0 pad_maximum_fusion
  5.1 7.3 %all-to-all-start = ((bf16[16,19,1024]{2,1,0:T(8,128)(2,1)}), bf16[16,19,1024]{2,1,0:T(8,128)(2,1)S(1)}, u32[]{:S(2)}, u32[]{:S(2)}) async-start(bf16[16,19,1024]{2,1,0:T(8,128)(2,1)} %pad_maximum_fusion), calls=%async_computation | async-start | bytes 1572864 | tf_op jit(solution)/shard_map/all_to_all | solution.py:98
  12.4 0.0 copy-done
  12.5 0.1 copy.9
  12.6 12.9 %all-to-all-done.rows_ref = bf16[16,19,1024]{2,1,0:T(8,128)(2,1)S(1)} async-done(((bf16[16,19,1024]{2,1,0:T(8,128)(2,1)}), bf16[16,19,1024]{2,1,0:T(8,128)(2,1)S(1)}, u32[]{:S(2)}, u32[]{:S(2)}) %all-to-all-start) | async-done | bytes 622624 | tf_op jit(solution)/shard_map/all_to_all | solution.py:98
  25.4 77.4 %shard_map.68 = f32[16,32]{1,0:T(8,128)} custom-call(bf16[16,19,1024]{2,1,0:T(8,128)(2,1)S(1)} %all-to-all-done.rows_ref, f32[256,16]{1,0:T(8,128)S(1)} %bitcast.3), custom_call_target="tpu_custom_call" | custom-call | tf_op jit(solution)/shard_map/pallas_call | solution.py:100
  102.8 0.7 reduce_max.9
  103.6 65.1 %pmax.7 = f32[32]{0:T(128)} all-reduce(f32[32]{0:T(128)S(1)} %reduce_max.9), channel_id=1, replica_groups=mesh['row'=16,'feat'=8] {'row','feat'}, use_global_device_ids=true, to_apply=%region_1.0 | all-reduce | flops 32 | bytes 256 | tf_op jit(solution)/shard_map/pmax | solution.py:112
  (6 shorter events, 0.1 us)
Async XLA Ops:
  0.6 11.8 %copy-start = (f32[256,256]{1,0:T(8,128)S(1)}, f32[256,256]{1,0:T(8,128)}, u32[]{:S(2)}) copy-start(f32[256,256]{1,0:T(8,128)} %param.6) | copy-start | bytes 786436
  5.1 20.3 %all-to-all-start = ((bf16[16,19,1024]{2,1,0:T(8,128)(2,1)}), bf16[16,19,1024]{2,1,0:T(8,128)(2,1)S(1)}, u32[]{:S(2)}, u32[]{:S(2)}) async-start(bf16[16,19,1024]{2,1,0:T(8,128)(2,1)} %pad_maximum_fusion), calls=%async_computation | async-start | bytes 1572864 | tf_op jit(solution)/shard_map/all_to_all | solution.py:98

commit v2 on v0

v2 whole, which is shorter than its diff:
```python
import jax
import jax.numpy as jnp
from jax import lax
from jax.experimental import pallas as pl
from jax.experimental.pallas import tpu as pltpu
from jax.sharding import PartitionSpec as P

NODES = 32
PENALTY = 1.0
LANES = 128
COARSE = 8
FINE = 32
PIECE = 32


def dot_nt(left, right):
    return lax.dot_general(
        left, right, (((1,), (1,)), ((), ())), preferred_element_type=jnp.float32
    )


def iota(shape, axis):
    return lax.broadcasted_iota(jnp.int32, shape, axis)


def sort_kernel(value_ref, grad_ref, hess_ref, node_ref, sent_ref):
    rows, feats = value_ref.shape
    parts = sent_ref.shape[0]
    own = feats // parts
    chunks = rows // LANES
    node = node_ref[...]
    member = (jnp.broadcast_to(node, (NODES, rows)) == iota((NODES, rows), 0)).astype(jnp.float32)
    earlier = (jnp.broadcast_to(node, (NODES, rows)) < iota((NODES, rows), 0)).astype(jnp.float32)
    upper = (iota((LANES, LANES), 0) <= iota((LANES, LANES), 1)).astype(jnp.bfloat16)
    offset = jnp.sum(earlier, axis=1, keepdims=True)
    ranks = []
    for c in range(chunks):
        piece = member[:, c * LANES : (c + 1) * LANES]
        running = jnp.dot(piece.astype(jnp.bfloat16), upper, preferred_element_type=jnp.float32)
        ranks.append(jnp.sum(piece * (running + (offset - 1.0)), axis=0, keepdims=True))
        offset = offset + jnp.sum(piece, axis=1, keepdims=True)
    rank = jnp.concatenate(ranks, axis=1).astype(jnp.int32)

    side = jnp.concatenate(
        [grad_ref[...], hess_ref[...], node.astype(jnp.float32), jnp.zeros((13, rows), jnp.float32)],
        axis=0,
    ).astype(jnp.bfloat16)
    operand = jnp.concatenate([value_ref[...].T, side], axis=0)
    block = 2 * LANES
    sides = []
    for b in range(rows // block):
        chosen = jnp.where(
            jnp.broadcast_to(rank, (block, rows)) == iota((block, rows), 0) + b * block, 1.0, 0.0
        ).astype(jnp.bfloat16)
        moved = dot_nt(operand, chosen)
        for half in range(2):
            c = 2 * b + half
            lanes = slice(half * LANES, (half + 1) * LANES)
            sent_ref[:, c * own : (c + 1) * own, :] = (
                moved[:feats, lanes].astype(jnp.bfloat16).reshape(parts, own, LANES)
            )
            sides.append(moved[feats : feats + 3, lanes])
    packed = jnp.concatenate(
        [sides[c][i : i + 1] for i in range(3) for c in range(chunks)], axis=0
    ).astype(jnp.bfloat16)
    for d in range(parts):
        sent_ref[d, chunks * own :, :] = packed


def gain_kernel(
    sent_ref, edge_ref, gain_ref, best_ref,
    side_ref, fine_ref, coarse_ref, side_tile_ref, stat_ref, wide_ref, hist_ref, total_ref, top_ref,
):
    parts = sent_ref.shape[0]
    feats, bins = edge_ref.shape
    chunks = (sent_ref.shape[1] - 24) // feats
    per_vector = LANES // PIECE
    tiles, _, tile_rows = fine_ref.shape
    groups = stat_ref.shape[0]
    group_feats = feats // groups

    hist_ref[...] = jnp.zeros_like(hist_ref)
    total_ref[...] = jnp.zeros_like(total_ref)
    for s in range(parts):
        side_ref[s] = sent_ref[s, chunks * feats :, :].astype(jnp.float32)

    edges = edge_ref[...]
    low_edges, high_edges = edges[:, :LANES], edges[:, LANES:]
    lane = iota((feats, LANES), 1)
    coarse_edges = [
        jnp.broadcast_to(edges[:, h * FINE : h * FINE + 1], (feats, LANES)) for h in range(COARSE)
    ]

    def search(value):
        coarse = jnp.full((feats, LANES), -1, jnp.int32)
        for h in range(COARSE):
            coarse = coarse + jnp.where(value >= coarse_edges[h], 1, 0)
        base = jnp.maximum(coarse, 0) * FINE
        is_high = base >= LANES
        base = jnp.where(is_high, base - LANES, base)
        place = base
        step = FINE // 2
        while step >= 1:
            probe = place + step
            edge = jnp.where(
                is_high,
                jnp.take_along_axis(high_edges, probe, axis=1),
                jnp.take_along_axis(low_edges, probe, axis=1),
            )
            place = jnp.where(value >= edge, probe, place)
            step //= 2
        return coarse.astype(jnp.float32), (place - base).astype(jnp.float32)

    block_of = lane // PIECE
    block_row = iota((1, LANES), 1) // PIECE

    def shuffle(pieces, blocks):
        outs = []
        for j in range(per_vector):
            out = None
            for s in range(per_vector):
                shift = ((s - j) * PIECE) % LANES
                moved = pieces[s] if shift == 0 else pltpu.roll(pieces[s], shift, 1)
                out = moved if out is None else jnp.where(blocks == s, moved, out)
            outs.append(out)
        return outs

    @pl.loop(0, chunks)
    def _(c):
        for q in range(parts // per_vector):
            fines, coarses, sides = [], [], []
            for s in range(q * per_vector, (q + 1) * per_vector):
                value = sent_ref[s, pl.ds(pl.multiple_of(c * feats, feats), feats), :].astype(
                    jnp.float32
                )
                coarse, fine = search(value)
                coarses.append(coarse)
                fines.append(fine)
                sides.append([side_ref[s, pl.ds(8 * i + c, 1), :] for i in range(3)])
            lanes = slice(q * LANES, (q + 1) * LANES)
            for j, out in enumerate(shuffle(fines, block_of)):
                fine_ref[c * per_vector + j, :, lanes] = out
            for j, out in enumerate(shuffle(coarses, block_of)):
                coarse_ref[c * per_vector + j, :, lanes] = out
            for i in range(3):
                for j, out in enumerate(shuffle([side[i] for side in sides], block_row)):
                    side_tile_ref[c * per_vector + j, i : i + 1, lanes] = out

    fine_index = iota((FINE, tile_rows), 0).astype(jnp.float32).astype(jnp.bfloat16)
    coarse_index = (iota((2 * COARSE, tile_rows), 0) % COARSE).astype(jnp.float32).astype(jnp.bfloat16)
    is_grad = iota((2 * COARSE, tile_rows), 0) < COARSE
    quarter = iota((2 * COARSE, LANES), 1) // FINE
    zero = jnp.bfloat16(0)
    one = jnp.bfloat16(1)

    @pl.loop(0, tiles)
    def _(t):
        for f in range(feats):
            g, i = f // group_feats, f % group_feats
            fine = fine_ref[t, f : f + 1, :]
            fine = jnp.broadcast_to(fine, (FINE, tile_rows)).astype(jnp.bfloat16)
            stat_ref[g, i * FINE : (i + 1) * FINE, :] = jnp.where(fine <= fine_index, one, zero)
            coarse = coarse_ref[t, f : f + 1, :]
            wide_ref[f] = jnp.broadcast_to(coarse, (2 * COARSE, tile_rows)).astype(jnp.bfloat16)
        grad = side_tile_ref[t, 0:1, :]
        hess = side_tile_ref[t, 1:2, :]
        node = side_tile_ref[t, 2:3, :]
        first = jnp.min(node).astype(jnp.int32)
        last = jnp.max(node).astype(jnp.int32)
        both = jnp.where(
            is_grad,
            jnp.broadcast_to(grad, (2 * COARSE, tile_rows)),
            jnp.broadcast_to(hess, (2 * COARSE, tile_rows)),
        )
        node_wide = jnp.broadcast_to(node, (2 * COARSE, tile_rows))

        @pl.loop(first, last + 1)
        def _(n):
            masked = jnp.where(node_wide == n.astype(jnp.float32), both, 0.0)
            partial = masked[:, :LANES]
            for k in range(1, tile_rows // LANES):
                partial = partial + masked[:, k * LANES : (k + 1) * LANES]
            total_ref[n] += partial
            masked = masked.astype(jnp.bfloat16)
            for g in range(groups):
                stream = jnp.concatenate(
                    [
                        jnp.where(wide_ref[g * group_feats + i] == coarse_index, masked, zero)
                        for i in range(group_feats)
                    ],
                    axis=0,
                )
                product = dot_nt(stream, stat_ref[g])
                for half in range(2):
                    picked = product[64 * half : 64 * half + 64, 128 * half : 128 * half + 128]
                    packed = picked[:16]
                    for i in range(1, 4):
                        packed = jnp.where(quarter == i, picked[16 * i : 16 * i + 16], packed)
                    hist_ref[n, 2 * g + half] += packed

    row = iota((COARSE, LANES), 0)
    last_lane = iota((COARSE, LANES), 1) | (FINE - 1)

    def left_sums(part):
        ends = jnp.take_along_axis(part, last_lane, axis=1)
        shift = 1
        while shift < COARSE:
            ends = ends + jnp.where(row >= shift, pltpu.roll(ends, shift, 0), 0.0)
            shift *= 2
        return part + jnp.where(row >= 1, pltpu.roll(ends, 1, 0), 0.0)

    @pl.loop(0, NODES)
    def _(n):
        sums = jnp.sum(total_ref[n], axis=1, keepdims=True)
        grad_total = jnp.broadcast_to(sums[0:1], (COARSE, LANES))
        hess_total = jnp.broadcast_to(sums[COARSE : COARSE + 1], (COARSE, LANES))
        whole = jnp.square(grad_total) / (hess_total + PENALTY)
        for q in range(feats // 4):
            part = hist_ref[n, q]
            grad_left = left_sums(part[:COARSE])
            hess_left = left_sums(part[COARSE:])
            split = jnp.square(grad_left) / (hess_left + PENALTY)
            split = split + jnp.square(grad_total - grad_left) / (hess_total - hess_left + PENALTY)
            split = split - whole
            top_ref[q, pl.ds(n, 1), :] = jnp.max(split, axis=0, keepdims=True)

    best = None
    for q in range(feats // 4):
        top = top_ref[q]
        shift = FINE // 2
        while shift >= 1:
            top = jnp.maximum(top, pltpu.roll(top, LANES - shift, 1))
            shift //= 2
        turned = top.T
        for i in range(4):
            found = turned[FINE * i : FINE * i + 1]
            gain_ref[4 * q + i : 4 * q + i + 1] = found
            best = found if best is None else jnp.maximum(best, found)
    best_ref[...] = jnp.broadcast_to(best, best_ref.shape)


def on_device(features, cut_points, grad, hess, node_ids):
    parts = lax.axis_size("row")
    others = parts * lax.axis_size("feat")
    rows, feats = features.shape
    own = feats // parts
    bins = cut_points.shape[1]
    length = (own + 3) * rows // LANES
    in_vmem = pl.BlockSpec(memory_space=pltpu.VMEM)
    sent = pl.pallas_call(
        sort_kernel,
        out_shape=jax.ShapeDtypeStruct((parts, length, LANES), jnp.bfloat16),
        in_specs=[in_vmem] * 4,
        out_specs=in_vmem,
        name="sort_rows",
        compiler_params=pltpu.CompilerParams(vmem_limit_bytes=30 << 20),
    )(features, grad[None], hess[None], node_ids[None])
    gathered = lax.all_to_all(sent, "row", 0, 0)
    edges = lax.dynamic_slice_in_dim(cut_points, lax.axis_index("row") * own, own, 0)
    tile_rows = PIECE * parts
    tiles = rows // PIECE
    feature_gain, best = pl.pallas_call(
        gain_kernel,
        out_shape=(
            jax.ShapeDtypeStruct((own, NODES), jnp.float32),
            jax.ShapeDtypeStruct((others, NODES), jnp.float32),
        ),
        in_specs=[in_vmem] * 2,
        out_specs=(in_vmem, in_vmem),
        scratch_shapes=[
            pltpu.VMEM((parts, 24, LANES), jnp.float32),
            pltpu.VMEM((tiles, own, tile_rows), jnp.float32),
            pltpu.VMEM((tiles, own, tile_rows), jnp.float32),
            pltpu.VMEM((tiles, 8, tile_rows), jnp.float32),
            pltpu.VMEM((2, 256, tile_rows), jnp.bfloat16),
            pltpu.VMEM((own, 2 * COARSE, tile_rows), jnp.bfloat16),
            pltpu.VMEM((NODES, own // 4, 2 * COARSE, LANES), jnp.float32),
            pltpu.VMEM((NODES, 2 * COARSE, LANES), jnp.float32),
            pltpu.VMEM((own // 4, NODES, LANES), jnp.float32),
        ],
        name="split_gain",
        compiler_params=pltpu.CompilerParams(vmem_limit_bytes=40 << 20),
    )(gathered, edges)
    node_best = jnp.max(lax.all_to_all(best, ("row", "feat"), 0, 0), axis=0)
    return (feature_gain, node_best)


def solution(mesh):
    placed = (P("row", "feat"), P("feat", None), P("row"), P("row"), P("row"))
    return jax.shard_map(
        on_device,
        mesh=mesh,
        in_specs=placed,
        out_specs=(P(("feat", "row"), None), P()),
        check_vma=False,
    )
```

time: 414 us -> 112 us (0.27)
  waiting for transfers between devices: 169 us -> 11 us
  matrix products: 97 us -> 0 us
  blocking collectives: 94.8 us -> 17 us
  Pallas kernels: 0 us -> 73 us
  other arithmetic: 20.8 us -> 0.66 us
  between operations: 14.1 us -> 0.66 us
  local copies, waits for them, and re-layouts: 16.2 us -> 3.15 us
  starting transfers between devices: 0.04 us -> 7.34 us
    psum x1 -> x0, waiting for transfers between devices: 169 us -> none  [on_device(): summed = lax.psum(onehot_hist(features, cut_points, weights), 'row')]
    dot_general x16 -> x0, matrix products: 97 us -> none  [accumulate(): jnp.einsum('rfb,rk->fbk', indicator, piece_weights, preferred_element_typ...]
    pallas_call x0 -> x2, Pallas kernels: none -> 73 us  [the longest x1 71.3 us: on_device(): pl.pallas_call(gain_kernel, out_shape=(jax.ShapeDtypeStruct((own, NODES),...]
    pmax x1 -> x0, blocking collectives: 65.9 us -> none  [on_device(): node_best = lax.pmax(jnp.max(feature_gain, axis=0), ('row', 'feat'))]
    psum x1 -> x0, blocking collectives: 28.8 us -> none  [on_device(): totals = lax.psum(jnp.sum(weights.astype(jnp.float32), axis=0), 'row')]
    another operation x5 -> x0, other arithmetic: 19.3 us -> none
    all_to_all x0 -> x1, blocking collectives: none -> 17 us  [on_device(): node_best = jnp.max(lax.all_to_all(best, ('row', 'feat'), 0, 0), axis=0)]
    lt x16 -> x0, local copies, waits for them, and re-layouts: 11.5 us -> none  [accumulate(): valued < upper_bound[None]]
where the time goes in v2:
time: 112 us; the launch traced here: 113 us
  Pallas kernels  73 us (65%)
  blocking collectives  17 us (15%)
  waiting for transfers between devices  11 us (10%)
  starting transfers between devices  7.34 us (7%)
  local copies, waits for them, and re-layouts  3.15 us (3%)
    pallas_call x1, Pallas kernels, on_device(): pl.pallas_call(gain_kernel, out_shape=(jax.ShapeDtypeStruct((own, NODES),...  71.3 us
    all_to_all x1, blocking collectives, on_device(): node_best = jnp.max(lax.all_to_all(best, ('row', 'feat'), 0, 0), axis=0)  17 us
    all_to_all x1, waiting for transfers between devices, on_device(): gathered = lax.all_to_all(sent, 'row', 0, 0)  11 us
    all_to_all x1, starting transfers between devices, on_device(): gathered = lax.all_to_all(sent, 'row', 0, 0)  7.34 us
    unnamed x10, local copies, waits for them, and re-layouts  3.15 us
  transfers between devices with their start and end apart: 1, of which 1 were waited for; matrix products, arithmetic and copies ran while one was open for 0% of the time, Pallas kernels for 0%

profile of v2, /device:TPU:1, one launch (start us, length us, event | category | flops | bytes accessed | tf_op | source)
XLA Modules:
  0.0 112.9 jit_solution(5181186016407095401)
XLA Ops:
  0.6 0.0 copy-start
  0.6 0.0 copy-start.2
  0.7 0.7 copy-done.2
  1.4 0.0 copy-start.1
  1.4 1.0 copy-done.1
  2.4 0.0 copy-start.3
  2.4 0.7 copy-done.3
  3.1 0.0 copy-start.4
  3.1 0.7 copy-done.4
  3.8 1.8 %sort_rows.1 = bf16[16,152,128]{2,1,0:T(8,128)(2,1)} custom-call(bf16[1024,256]{1,0:T(8,128)(2,1)S(1)} %copy-done.1, f32[1,1024]{1,0:T(1,128)S(1)} %bitcast.7, f32[1,1024]{1,0:T(1,128)S(1)} %bitcast.8, s32[1,1024]{1,0:T(1,128)S(1)} %bitcast.9), custom_call_target="tpu_custom_call" | custom-call | tf_op jit(solution)/shard_map/sort_rows/pallas_call | solution.py:250
  5.6 7.3 %all-to-all-start = ((bf16[16,152,128]{2,1,0:T(8,128)(2,1)}), bf16[16,152,128]{2,1,0:T(8,128)(2,1)S(1)}, u32[]{:S(2)}, u32[]{:S(2)}) async-start(bf16[16,152,128]{2,1,0:T(8,128)(2,1)} %sort_rows.1), calls=%async_computation | async-start | bytes 1245184 | tf_op jit(solution)/shard_map/all_to_all | solution.py:258
  12.9 0.0 copy-done
  12.9 11.0 %all-to-all-done.sent_ref = bf16[16,152,128]{2,1,0:T(8,128)(2,1)S(1)} async-done(((bf16[16,152,128]{2,1,0:T(8,128)(2,1)}), bf16[16,152,128]{2,1,0:T(8,128)(2,1)S(1)}, u32[]{:S(2)}, u32[]{:S(2)}) %all-to-all-start) | async-done | bytes 622624 | tf_op jit(solution)/shard_map/all_to_all | solution.py:258
  23.9 71.3 %split_gain.1 = (f32[16,32]{1,0:T(8,128)}, f32[128,32]{1,0:T(8,128)S(1)}) custom-call(bf16[16,152,128]{2,1,0:T(8,128)(2,1)S(1)} %all-to-all-done.sent_ref, f32[16,256]{1,0:T(8,128)S(1)} %constant_dynamic-slice_fusion.edge_ref), custom_call_target="tpu_custom_call" | custom-call | tf_op jit(solution)/shard_map/split_gain/pallas_call | solution.py:262
  95.2 17.0 %all_to_all.14 = f32[128,1,32]{2,1,0:T(1,128)S(1)} all-to-all(f32[128,1,32]{2,1,0:T(1,128)S(1)} %bitcast.6), channel_id=1, replica_groups=mesh['row'=16,'feat'=8] {'row','feat'}, dimensions={0} | all-to-all | bytes 32768 | tf_op jit(solution)/shard_map/all_to_all | solution.py:284
  112.2 0.7 reduce_max.9
  (1 shorter events, 0.0 us)
Async XLA Ops:
  0.6 12.3 %copy-start = (f32[256,256]{1,0:T(8,128)S(1)}, f32[256,256]{1,0:T(8,128)}, u32[]{:S(2)}) copy-start(f32[256,256]{1,0:T(8,128)} %param.6) | copy-start | bytes 786436
  0.6 0.7 copy-start.2
  1.4 1.0 copy-start.1
  2.4 0.7 copy-start.3
  3.1 0.7 copy-start.4
  5.6 18.4 %all-to-all-start = ((bf16[16,152,128]{2,1,0:T(8,128)(2,1)}), bf16[16,152,128]{2,1,0:T(8,128)(2,1)S(1)}, u32[]{:S(2)}, u32[]{:S(2)}) async-start(bf16[16,152,128]{2,1,0:T(8,128)(2,1)} %sort_rows.1), calls=%async_computation | async-start | bytes 1245184 | tf_op jit(solution)/shard_map/all_to_all | solution.py:258

commit v3 on v2

v3 whole, which is shorter than its diff:
```python
import jax
import jax.numpy as jnp
from jax import lax
from jax.experimental import pallas as pl
from jax.experimental.pallas import tpu as pltpu
from jax.sharding import PartitionSpec as P

NODES = 32
PENALTY = 1.0
LANES = 128
COARSE = 8
FINE = 32
PIECE = 16
QUAD = 4
NODE_BLOCK = 4
UNROLL = 2


def dot_nt(left, right):
    return lax.dot_general(
        left, right, (((1,), (1,)), ((), ())), preferred_element_type=jnp.float32
    )


def iota(shape, axis):
    return lax.broadcasted_iota(jnp.int32, shape, axis)


def sort_kernel(value_ref, grad_ref, hess_ref, node_ref, sent_ref):
    rows, feats = value_ref.shape
    parts = sent_ref.shape[0]
    own = feats // parts
    chunks = rows // LANES
    node = node_ref[...]
    member = (jnp.broadcast_to(node, (NODES, rows)) == iota((NODES, rows), 0)).astype(jnp.float32)
    earlier = (jnp.broadcast_to(node, (NODES, rows)) < iota((NODES, rows), 0)).astype(jnp.float32)
    upper = (iota((LANES, LANES), 0) <= iota((LANES, LANES), 1)).astype(jnp.bfloat16)
    offset = jnp.sum(earlier, axis=1, keepdims=True)
    ranks = []
    for c in range(chunks):
        piece = member[:, c * LANES : (c + 1) * LANES]
        running = jnp.dot(piece.astype(jnp.bfloat16), upper, preferred_element_type=jnp.float32)
        ranks.append(jnp.sum(piece * (running + (offset - 1.0)), axis=0, keepdims=True))
        offset = offset + jnp.sum(piece, axis=1, keepdims=True)
    rank = jnp.concatenate(ranks, axis=1).astype(jnp.int32)

    side = jnp.concatenate(
        [grad_ref[...], hess_ref[...], node.astype(jnp.float32), jnp.zeros((13, rows), jnp.float32)],
        axis=0,
    ).astype(jnp.bfloat16)
    operand = jnp.concatenate([value_ref[...].T, side], axis=0)
    block = 2 * LANES
    sides = []
    for b in range(rows // block):
        chosen = jnp.where(
            jnp.broadcast_to(rank, (block, rows)) == iota((block, rows), 0) + b * block, 1.0, 0.0
        ).astype(jnp.bfloat16)
        moved = dot_nt(operand, chosen)
        for half in range(2):
            c = 2 * b + half
            lanes = slice(half * LANES, (half + 1) * LANES)
            sent_ref[:, c * own : (c + 1) * own, :] = (
                moved[:feats, lanes].astype(jnp.bfloat16).reshape(parts, own, LANES)
            )
            sides.append(moved[feats : feats + 3, lanes])
    packed = jnp.concatenate(
        [sides[c][i : i + 1] for i in range(3) for c in range(chunks)], axis=0
    ).astype(jnp.bfloat16)
    for d in range(parts):
        sent_ref[d, chunks * own :, :] = packed


def search_tables(edges):
    feats = edges.shape[0]
    lane = iota((feats, LANES), 1)
    low, high = edges[:, :LANES], edges[:, LANES:]

    def pick(index):
        place = jnp.where(index >= LANES, index - LANES, index)
        return jnp.where(
            index >= LANES,
            jnp.take_along_axis(high, place, axis=1),
            jnp.take_along_axis(low, place, axis=1),
        )

    inner = jnp.zeros((feats, LANES), jnp.int32)
    for level in range(7):
        start = 1 << level
        inner = jnp.where(lane >= start, (2 * (lane - start) + 1) * (1 << (7 - level)), inner)
    return pick(inner), pick(2 * lane + 1)


def gain_kernel(
    sent_ref, edge_ref, gain_ref, best_ref,
    side_ref, fine_ref, coarse_ref, side_tile_ref, stat_ref, wide_ref, hist_ref, total_ref, top_ref,
):
    parts = sent_ref.shape[0]
    feats, bins = edge_ref.shape
    chunks = (sent_ref.shape[1] - 24) // feats
    per_vector = LANES // PIECE
    tiles, _, tile_rows = fine_ref.shape
    quads = feats // QUAD

    hist_ref[...] = jnp.zeros_like(hist_ref)
    total_ref[...] = jnp.zeros_like(total_ref)
    for s in range(parts):
        side_ref[s] = sent_ref[s, chunks * feats :, :].astype(jnp.float32)

    edges = edge_ref[...]
    inner, leaf = search_tables(edges)

    def edge_at(j):
        return jnp.broadcast_to(edges[:, j : j + 1], (feats, LANES))

    lowest = edge_at(0)
    steps = [edge_at(32 * h) for h in range(8)]

    def search(value):
        b0 = value >= steps[4]
        b1 = value >= jnp.where(b0, steps[6], steps[2])
        e0 = jnp.where(b1, steps[3], steps[1])
        e1 = jnp.where(b1, steps[7], steps[5])
        b2 = value >= jnp.where(b0, e1, e0)
        place = jnp.where(b0, 12, 8) + jnp.where(b1, 2, 0) + jnp.where(b2, 1, 0)
        for level in range(3, 8):
            if level < 7:
                edge = jnp.take_along_axis(inner, place, axis=1)
            else:
                edge = jnp.take_along_axis(leaf, place - LANES, axis=1)
            place = 2 * place + jnp.where(value >= edge, 1, 0)
        return jnp.where(value >= lowest, place - 256, -1)

    def shuffle(pieces, block):
        pieces = list(pieces)
        step = per_vector // 2
        while step >= 1:
            keep = (block & step) == 0
            for s in range(per_vector):
                if s & step == 0:
                    a, b = pieces[s], pieces[s + step]
                    pieces[s] = jnp.where(keep, a, pltpu.roll(b, step * PIECE, 1))
                    pieces[s + step] = jnp.where(keep, pltpu.roll(a, LANES - step * PIECE, 1), b)
            step //= 2
        return pieces

    block = iota((feats, LANES), 1) // PIECE
    block_side = iota((3, LANES), 1) // PIECE

    @pl.loop(0, chunks)
    def _(c):
        for q in range(parts // per_vector):
            slots, sides = [], []
            for s in range(q * per_vector, (q + 1) * per_vector):
                value = sent_ref[s, pl.ds(pl.multiple_of(c * feats, feats), feats), :]
                slots.append(search(value.astype(jnp.float32)))
                sides.append(side_ref[s, pl.ds(c, 3, stride=8), :])
            lanes = slice(q * LANES, (q + 1) * LANES)
            for j, slot in enumerate(shuffle(slots, block)):
                coarse = slot >> 5
                coarse_ref[c * per_vector + j, :, lanes] = coarse.astype(jnp.float32)
                fine_ref[c * per_vector + j, :, lanes] = (slot & 31).astype(jnp.float32)
            for j, side in enumerate(shuffle(sides, block_side)):
                side_tile_ref[c * per_vector + j, 0:3, lanes] = side

    fine_index = iota((FINE, tile_rows), 0).astype(jnp.float32).astype(jnp.bfloat16)
    coarse_index = (iota((2 * COARSE, tile_rows), 0) & (COARSE - 1)).astype(jnp.float32)
    coarse_index = coarse_index.astype(jnp.bfloat16)
    is_grad = iota((2 * COARSE, tile_rows), 0) < COARSE
    quarter = iota((2 * COARSE, LANES), 1) // FINE
    zero = jnp.bfloat16(0)
    one = jnp.bfloat16(1)
    deep = 2 * COARSE

    def node_block(u, q, first, count, node_wide, both, with_total):
        masked = []
        for b in range(count):
            m = jnp.where(node_wide == (first + b).astype(jnp.float32), both, 0.0)
            if with_total:
                partial = m[:, :LANES]
                for k in range(1, tile_rows // LANES):
                    partial = partial + m[:, k * LANES : (k + 1) * LANES]
                total_ref[first + b] += partial
            masked.append(m.astype(jnp.bfloat16))
        return masked

    def add_product(u, q, first, masked):
        here = [wide_ref[u, q * QUAD + i] == coarse_index for i in range(QUAD)]
        stream = jnp.concatenate(
            [jnp.where(here[i], m, zero) for m in masked for i in range(QUAD)], axis=0
        )
        product = dot_nt(stream, stat_ref[u, q])
        for b in range(len(masked)):
            at = b * QUAD * deep
            packed = product[at : at + deep]
            for i in range(1, QUAD):
                packed = jnp.where(
                    quarter == i, product[at + deep * i : at + deep * (i + 1)], packed
                )
            hist_ref[first + b, q] += packed

    @pl.loop(0, tiles // UNROLL)
    def _(p):
        state = []
        for u in range(UNROLL):
            t = p * UNROLL + u
            grad = side_tile_ref[t, 0:1, :]
            hess = side_tile_ref[t, 1:2, :]
            node = side_tile_ref[t, 2:3, :]
            first = jnp.minimum(jnp.min(node).astype(jnp.int32), NODES - NODE_BLOCK)
            last = jnp.max(node).astype(jnp.int32)
            both = jnp.where(
                is_grad,
                jnp.broadcast_to(grad, (deep, tile_rows)),
                jnp.broadcast_to(hess, (deep, tile_rows)),
            )
            node_wide = jnp.broadcast_to(node, (deep, tile_rows))
            state.append((t, first, last, both, node_wide))
        for u in range(UNROLL):
            t, first, last, both, node_wide = state[u]
            masked = node_block(u, 0, first, NODE_BLOCK, node_wide, both, True)
            for q in range(quads):
                for i in range(QUAD):
                    f = q * QUAD + i
                    fine = jnp.broadcast_to(fine_ref[t, f : f + 1, :], (FINE, tile_rows))
                    stat_ref[u, q, i * FINE : (i + 1) * FINE, :] = jnp.where(
                        fine.astype(jnp.bfloat16) <= fine_index, one, zero
                    )
                    coarse = jnp.broadcast_to(coarse_ref[t, f : f + 1, :], (deep, tile_rows))
                    wide_ref[u, f] = coarse.astype(jnp.bfloat16)
                add_product(u, q, first, masked)
        for u in range(UNROLL):
            t, first, last, both, node_wide = state[u]

            @pl.loop(first + NODE_BLOCK, last + 1)
            def _(n):
                masked = node_block(u, 0, n, 1, node_wide, both, True)
                for q in range(quads):
                    add_product(u, q, n, masked)

    row = iota((COARSE, LANES), 0)
    last_lane = iota((COARSE, LANES), 1) | (FINE - 1)

    def left_sums(part):
        ends = jnp.take_along_axis(part, last_lane, axis=1)
        shift = 1
        while shift < COARSE:
            ends = ends + jnp.where(row >= shift, pltpu.roll(ends, shift, 0), 0.0)
            shift *= 2
        return part + jnp.where(row >= 1, pltpu.roll(ends, 1, 0), 0.0)

    @pl.loop(0, NODES // 2)
    def _(pair):
        for k in range(2):
            n = 2 * pair + k
            sums = jnp.sum(total_ref[n], axis=1, keepdims=True)
            grad_total = jnp.broadcast_to(sums[0:1], (COARSE, LANES))
            hess_total = jnp.broadcast_to(sums[COARSE : COARSE + 1], (COARSE, LANES))
            whole = jnp.square(grad_total) / (hess_total + PENALTY)
            for q in range(quads):
                part = hist_ref[n, q]
                grad_left = left_sums(part[:COARSE])
                hess_left = left_sums(part[COARSE:])
                split = jnp.square(grad_left) / (hess_left + PENALTY)
                split = split + jnp.square(grad_total - grad_left) / (
                    hess_total - hess_left + PENALTY
                )
                split = split - whole
                top_ref[q, pl.ds(n, 1), :] = jnp.max(split, axis=0, keepdims=True)

    best = None
    for q in range(quads):
        top = top_ref[q]
        shift = FINE // 2
        while shift >= 1:
            top = jnp.maximum(top, pltpu.roll(top, LANES - shift, 1))
            shift //= 2
        turned = top.T
        for i in range(QUAD):
            found = turned[FINE * i : FINE * i + 1]
            gain_ref[QUAD * q + i : QUAD * q + i + 1] = found
            best = found if best is None else jnp.maximum(best, found)
    best_ref[...] = jnp.broadcast_to(best, best_ref.shape)


def on_device(features, cut_points, grad, hess, node_ids):
    parts = lax.axis_size("row")
    others = parts * lax.axis_size("feat")
    rows, feats = features.shape
    own = feats // parts
    bins = cut_points.shape[1]
    length = (own + 3) * rows // LANES
    in_vmem = pl.BlockSpec(memory_space=pltpu.VMEM)
    sent = pl.pallas_call(
        sort_kernel,
        out_shape=jax.ShapeDtypeStruct((parts, length, LANES), jnp.bfloat16),
        in_specs=[in_vmem] * 4,
        out_specs=in_vmem,
        name="sort_rows",
        compiler_params=pltpu.CompilerParams(vmem_limit_bytes=30 << 20),
    )(features, grad[None], hess[None], node_ids[None])
    gathered = lax.all_to_all(sent, "row", 0, 0)
    edges = lax.dynamic_slice_in_dim(cut_points, lax.axis_index("row") * own, own, 0)
    tile_rows = PIECE * parts
    tiles = rows // PIECE
    feature_gain, best = pl.pallas_call(
        gain_kernel,
        out_shape=(
            jax.ShapeDtypeStruct((own, NODES), jnp.float32),
            jax.ShapeDtypeStruct((others, NODES), jnp.float32),
        ),
        in_specs=[in_vmem] * 2,
        out_specs=(in_vmem, in_vmem),
        scratch_shapes=[
            pltpu.VMEM((parts, 24, LANES), jnp.float32),
            pltpu.VMEM((tiles, own, tile_rows), jnp.float32),
            pltpu.VMEM((tiles, own, tile_rows), jnp.float32),
            pltpu.VMEM((tiles, 8, tile_rows), jnp.float32),
            pltpu.VMEM((UNROLL, own // QUAD, QUAD * FINE, tile_rows), jnp.bfloat16),
            pltpu.VMEM((UNROLL, own, 2 * COARSE, tile_rows), jnp.bfloat16),
            pltpu.VMEM((NODES, own // QUAD, 2 * COARSE, LANES), jnp.float32),
            pltpu.VMEM((NODES, 2 * COARSE, LANES), jnp.float32),
            pltpu.VMEM((own // QUAD, NODES, LANES), jnp.float32),
        ],
        name="split_gain",
        compiler_params=pltpu.CompilerParams(vmem_limit_bytes=40 << 20),
    )(gathered, edges)
    node_best = jnp.max(lax.all_to_all(best, ("row", "feat"), 0, 0), axis=0)
    return (feature_gain, node_best)


def solution(mesh):
    placed = (P("row", "feat"), P("feat", None), P("row"), P("row"), P("row"))
    return jax.shard_map(
        on_device,
        mesh=mesh,
        in_specs=placed,
        out_specs=(P(("feat", "row"), None), P()),
        check_vma=False,
    )
```

time: 112 us -> 69.9 us (0.62); the launches traced: 113 us -> 69.5 us
  Pallas kernels: 73 us -> 29.7 us
    pallas_call x1, Pallas kernels: 71.3 us -> 27.9 us  [on_device(): pl.pallas_call(gain_kernel, out_shape=(jax.ShapeDtypeStruct((own, NODES),...]
where the time goes in v3:
time: 69.9 us; the launch traced here: 69.5 us
  Pallas kernels  29.7 us (42%)
  blocking collectives  17 us (24%)
  waiting for transfers between devices  11 us (16%)
  starting transfers between devices  7.34 us (11%)
  local copies, waits for them, and re-layouts  3.15 us (5%)
    pallas_call x1, Pallas kernels, on_device(): pl.pallas_call(gain_kernel, out_shape=(jax.ShapeDtypeStruct((own, NODES),...  27.9 us
    all_to_all x1, blocking collectives, on_device(): node_best = jnp.max(lax.all_to_all(best, ('row', 'feat'), 0, 0), axis=0)  17 us
    all_to_all x1, waiting for transfers between devices, on_device(): gathered = lax.all_to_all(sent, 'row', 0, 0)  11 us
    all_to_all x1, starting transfers between devices, on_device(): gathered = lax.all_to_all(sent, 'row', 0, 0)  7.34 us
    unnamed x10, local copies, waits for them, and re-layouts  3.15 us
    pallas_call x1, Pallas kernels, on_device(): pl.pallas_call(sort_kernel, out_shape=jax.ShapeDtypeStruct((parts, length...  1.77 us
  transfers between devices with their start and end apart: 1, of which 1 were waited for; matrix products, arithmetic and copies ran while one was open for 0% of the time, Pallas kernels for 0%

profile of v3, /device:TPU:1, one launch (start us, length us, event | category | flops | bytes accessed | tf_op | source)
XLA Modules:
  0.0 69.5 jit_solution(5825139042781405472)
XLA Ops:
  0.6 0.0 copy-start
  0.6 0.0 copy-start.2
  0.7 0.7 %copy-done.2 = f32[1024]{0:T(1024)S(1)} copy-done((f32[1024]{0:T(1024)S(1)}, f32[1024]{0:T(1024)}, u32[]{:S(2)}) %copy-start.2) | copy-done | bytes 4120
  1.4 0.0 copy-start.1
  1.4 1.0 %copy-done.1 = bf16[1024,256]{1,0:T(8,128)(2,1)S(1)} copy-done((bf16[1024,256]{1,0:T(8,128)(2,1)S(1)}, bf16[1024,256]{1,0:T(8,128)(2,1)}, u32[]{:S(2)}) %copy-start.1) | copy-done | bytes 524312
  2.4 0.0 copy-start.3
  2.4 0.7 copy-done.3
  3.1 0.0 copy-start.4
  3.1 0.7 copy-done.4
  3.8 1.8 %sort_rows.1 = bf16[16,152,128]{2,1,0:T(8,128)(2,1)} custom-call(bf16[1024,256]{1,0:T(8,128)(2,1)S(1)} %copy-done.1, f32[1,1024]{1,0:T(1,128)S(1)} %bitcast.7, f32[1,1024]{1,0:T(1,128)S(1)} %bitcast.8, s32[1,1024]{1,0:T(1,128)S(1)} %bitcast.9), custom_call_target="tpu_custom_call" | custom-call | tf_op jit(solution)/shard_map/sort_rows/pallas_call | solution.py:293
  5.6 7.3 %all-to-all-start = ((bf16[16,152,128]{2,1,0:T(8,128)(2,1)}), bf16[16,152,128]{2,1,0:T(8,128)(2,1)S(1)}, u32[]{:S(2)}, u32[]{:S(2)}) async-start(bf16[16,152,128]{2,1,0:T(8,128)(2,1)} %sort_rows.1), calls=%async_computation | async-start | bytes 1245184 | tf_op jit(solution)/shard_map/all_to_all | solution.py:301
  12.9 0.0 copy-done
  12.9 11.0 %all-to-all-done.sent_ref = bf16[16,152,128]{2,1,0:T(8,128)(2,1)S(1)} async-done(((bf16[16,152,128]{2,1,0:T(8,128)(2,1)}), bf16[16,152,128]{2,1,0:T(8,128)(2,1)S(1)}, u32[]{:S(2)}, u32[]{:S(2)}) %all-to-all-start) | async-done | bytes 622624 | tf_op jit(solution)/shard_map/all_to_all | solution.py:301
  23.9 27.9 %split_gain.1 = (f32[16,32]{1,0:T(8,128)}, f32[128,32]{1,0:T(8,128)S(1)}) custom-call(bf16[16,152,128]{2,1,0:T(8,128)(2,1)S(1)} %all-to-all-done.sent_ref, f32[16,256]{1,0:T(8,128)S(1)} %constant_dynamic-slice_fusion.edge_ref), custom_call_target="tpu_custom_call" | custom-call | tf_op jit(solution)/shard_map/split_gain/pallas_call | solution.py:305
  51.8 17.0 %all_to_all.14 = f32[128,1,32]{2,1,0:T(1,128)S(1)} all-to-all(f32[128,1,32]{2,1,0:T(1,128)S(1)} %bitcast.6), channel_id=1, replica_groups=mesh['row'=16,'feat'=8] {'row','feat'}, dimensions={0} | all-to-all | bytes 32768 | tf_op jit(solution)/shard_map/all_to_all | solution.py:327
  68.9 0.7 reduce_max.9
  (1 shorter events, 0.0 us)
Async XLA Ops:
  0.6 12.3 %copy-start = (f32[256,256]{1,0:T(8,128)S(1)}, f32[256,256]{1,0:T(8,128)}, u32[]{:S(2)}) copy-start(f32[256,256]{1,0:T(8,128)} %param.6) | copy-start | bytes 786436
  0.6 0.7 %copy-start.2 = (f32[1024]{0:T(1024)S(1)}, f32[1024]{0:T(1024)}, u32[]{:S(2)}) copy-start(f32[1024]{0:T(1024)} %param.7) | copy-start | bytes 12292
  1.4 1.0 %copy-start.1 = (bf16[1024,256]{1,0:T(8,128)(2,1)S(1)}, bf16[1024,256]{1,0:T(8,128)(2,1)}, u32[]{:S(2)}) copy-start(bf16[1024,256]{1,0:T(8,128)(2,1)} %value_ref.1) | copy-start | bytes 1572868
  2.4 0.7 copy-start.3
  3.1 0.7 copy-start.4
  5.6 18.4 %all-to-all-start = ((bf16[16,152,128]{2,1,0:T(8,128)(2,1)}), bf16[16,152,128]{2,1,0:T(8,128)(2,1)S(1)}, u32[]{:S(2)}, u32[]{:S(2)}) async-start(bf16[16,152,128]{2,1,0:T(8,128)(2,1)} %sort_rows.1), calls=%async_computation | async-start | bytes 1245184 | tf_op jit(solution)/shard_map/all_to_all | solution.py:301

commit v4 on v3

--- a/solution.py
+++ b/solution.py
@@ -10,10 +10,9 @@
 LANES = 128
 COARSE = 8
 FINE = 32
-PIECE = 16
+PIECE = 32
 QUAD = 4
 NODE_BLOCK = 4
-UNROLL = 2
 
 
 def dot_nt(left, right):
@@ -24,6 +23,10 @@
 
 def iota(shape, axis):
     return lax.broadcasted_iota(jnp.int32, shape, axis)
+
+
+def look_up(table, index):
+    return jnp.take_along_axis(table, index, axis=1, mode="promise_in_bounds")
 
 
 def sort_kernel(value_ref, grad_ref, hess_ref, node_ref, sent_ref):
@@ -79,8 +82,8 @@
         place = jnp.where(index >= LANES, index - LANES, index)
         return jnp.where(
             index >= LANES,
-            jnp.take_along_axis(high, place, axis=1),
-            jnp.take_along_axis(low, place, axis=1),
+            look_up(high, place),
+            look_up(low, place),
         )
 
     inner = jnp.zeros((feats, LANES), jnp.int32)
@@ -92,43 +95,65 @@
 
 def gain_kernel(
     sent_ref, edge_ref, gain_ref, best_ref,
-    side_ref, fine_ref, coarse_ref, side_tile_ref, stat_ref, wide_ref, hist_ref, total_ref, top_ref,
+    side_ref, wide_edge_ref, even_fine_ref, even_coarse_ref, even_side_ref,
+    odd_fine_ref, odd_coarse_ref, odd_side_ref,
+    stat_ref, wide_ref, hist_ref, total_ref, top_ref,
 ):
     parts = sent_ref.shape[0]
     feats, bins = edge_ref.shape
     chunks = (sent_ref.shape[1] - 24) // feats
     per_vector = LANES // PIECE
-    tiles, _, tile_rows = fine_ref.shape
+    tile_rows = even_fine_ref.shape[2]
     quads = feats // QUAD
 
     hist_ref[...] = jnp.zeros_like(hist_ref)
-    total_ref[...] = jnp.zeros_like(total_ref)
+    total = jnp.zeros((16, NODES), jnp.float32)
     for s in range(parts):
-        side_ref[s] = sent_ref[s, chunks * feats :, :].astype(jnp.float32)
+        side = sent_ref[s, chunks * feats :, :].astype(jnp.float32)
+        side_ref[s] = side
+        for c in range(0, chunks, 2):
+            grad, hess, node = [
+                jnp.concatenate([side[8 * i + c : 8 * i + c + 1], side[8 * i + c + 1 : 8 * i + c + 2]], axis=1)
+                for i in range(3)
+            ]
+            wide = (NODES, 2 * LANES)
+            member = jnp.where(
+                jnp.broadcast_to(node, wide) == iota(wide, 0).astype(jnp.float32), 1.0, 0.0
+            ).astype(jnp.bfloat16)
+            both = jnp.concatenate(
+                [jnp.broadcast_to(grad, (8, 2 * LANES)), jnp.broadcast_to(hess, (8, 2 * LANES))], axis=0
+            ).astype(jnp.bfloat16)
+            total = total + dot_nt(both, member)
+    spread = jnp.concatenate([total, jnp.zeros((16, LANES - NODES), jnp.float32)], axis=1)
+    for n in range(NODES):
+        total_ref[n] = jnp.broadcast_to(spread[:, n : n + 1], (16, LANES))
 
     edges = edge_ref[...]
     inner, leaf = search_tables(edges)
 
-    def edge_at(j):
-        return jnp.broadcast_to(edges[:, j : j + 1], (feats, LANES))
-
-    lowest = edge_at(0)
-    steps = [edge_at(32 * h) for h in range(8)]
+    for j in range(32):
+        wide_edge_ref[j] = jnp.broadcast_to(edges[:, 8 * j : 8 * j + 1], (feats, LANES))
 
     def search(value):
-        b0 = value >= steps[4]
-        b1 = value >= jnp.where(b0, steps[6], steps[2])
-        e0 = jnp.where(b1, steps[3], steps[1])
-        e1 = jnp.where(b1, steps[7], steps[5])
-        b2 = value >= jnp.where(b0, e1, e0)
-        place = jnp.where(b0, 12, 8) + jnp.where(b1, 2, 0) + jnp.where(b2, 1, 0)
-        for level in range(3, 8):
+        bits = []
+        for level in range(5):
+            choice = [wide_edge_ref[(2 * m + 1) << (4 - level)] for m in range(1 << level)]
+            for bit in reversed(bits):
+                choice = [
+                    jnp.where(bit, choice[2 * m + 1], choice[2 * m])
+                    for m in range(len(choice) // 2)
+                ]
+            bits.append(value >= choice[0])
+        place = jnp.where(bits[0], 48, 32)
+        for level in range(1, 5):
+            place = place + jnp.where(bits[level], 16 >> level, 0)
+        for level in range(5, 8):
             if level < 7:
-                edge = jnp.take_along_axis(inner, place, axis=1)
+                edge = look_up(inner, place)
             else:
-                edge = jnp.take_along_axis(leaf, place - LANES, axis=1)
-            place = 2 * place + jnp.where(value >= edge, 1, 0)
-        return jnp.where(value >= lowest, place - 256, -1)
+                edge = look_up(leaf, place - LANES)
+            place = place + place + jnp.where(value >= edge, 1, 0)
+        return jnp.where(value >= wide_edge_ref[0], place - 256, -1)
 
     def shuffle(pieces, block):
         pieces = list(pieces)
@@ -146,8 +171,7 @@
     block = iota((feats, LANES), 1) // PIECE
     block_side = iota((3, LANES), 1) // PIECE
 
-    @pl.loop(0, chunks)
-    def _(c):
+    def prepare(c, fine_ref, coarse_ref, side_tile_ref):
         for q in range(parts // per_vector):
             slots, sides = [], []
             for s in range(q * per_vector, (q + 1) * per_vector):
@@ -156,11 +180,10 @@
                 sides.append(side_ref[s, pl.ds(c, 3, stride=8), :])
             lanes = slice(q * LANES, (q + 1) * LANES)
             for j, slot in enumerate(shuffle(slots, block)):
-                coarse = slot >> 5
-                coarse_ref[c * per_vector + j, :, lanes] = coarse.astype(jnp.float32)
-                fine_ref[c * per_vector + j, :, lanes] = (slot & 31).astype(jnp.float32)
+                coarse_ref[j, :, lanes] = (slot >> 5).astype(jnp.float32)
+                fine_ref[j, :, lanes] = (slot & 31).astype(jnp.float32)
             for j, side in enumerate(shuffle(sides, block_side)):
-                side_tile_ref[c * per_vector + j, 0:3, lanes] = side
+                side_tile_ref[j, 0:3, lanes] = side
 
     fine_index = iota((FINE, tile_rows), 0).astype(jnp.float32).astype(jnp.bfloat16)
     coarse_index = (iota((2 * COARSE, tile_rows), 0) & (COARSE - 1)).astype(jnp.float32)
@@ -171,23 +194,15 @@
     one = jnp.bfloat16(1)
     deep = 2 * COARSE
 
-    def node_block(u, q, first, count, node_wide, both, with_total):
-        masked = []
-        for b in range(count):
-            m = jnp.where(node_wide == (first + b).astype(jnp.float32), both, 0.0)
-            if with_total:
-                partial = m[:, :LANES]
-                for k in range(1, tile_rows // LANES):
-                    partial = partial + m[:, k * LANES : (k + 1) * LANES]
-                total_ref[first + b] += partial
-            masked.append(m.astype(jnp.bfloat16))
-        return masked
+    def mask_nodes(first, count, node_wide, both):
+        return [
+            jnp.where(node_wide == (first + b).astype(jnp.float32).astype(jnp.bfloat16), both, zero)
+            for b in range(count)
+        ]
 
     def add_product(u, q, first, masked):
-        here = [wide_ref[u, q * QUAD + i] == coarse_index for i in range(QUAD)]
-        stream = jnp.concatenate(
-            [jnp.where(here[i], m, zero) for m in masked for i in range(QUAD)], axis=0
-        )
+        here = [wide_ref[u, q * QUAD + i] for i in range(QUAD)]
+        stream = jnp.concatenate([here[i] * m for m in masked for i in range(QUAD)], axis=0)
         product = dot_nt(stream, stat_ref[u, q])
         for b in range(len(masked)):
             at = b * QUAD * deep
@@ -198,63 +213,80 @@
                 )
             hist_ref[first + b, q] += packed
 
-    @pl.loop(0, tiles // UNROLL)
-    def _(p):
-        state = []
-        for u in range(UNROLL):
-            t = p * UNROLL + u
-            grad = side_tile_ref[t, 0:1, :]
-            hess = side_tile_ref[t, 1:2, :]
-            node = side_tile_ref[t, 2:3, :]
+    def tile_sides(side_tile_ref, u):
+        wide = (deep, tile_rows)
+        both = jnp.where(
+            is_grad,
+            jnp.broadcast_to(side_tile_ref[u, 0:1, :], wide),
+            jnp.broadcast_to(side_tile_ref[u, 1:2, :], wide),
+        ).astype(jnp.bfloat16)
+        node = side_tile_ref[u, 2:3, :]
+        return node, jnp.broadcast_to(node, wide).astype(jnp.bfloat16), both
+
+    def accumulate(fine_ref, coarse_ref, side_tile_ref):
+        ranges = []
+        for u in range(per_vector):
+            node = side_tile_ref[u, 2:3, :]
             first = jnp.minimum(jnp.min(node).astype(jnp.int32), NODES - NODE_BLOCK)
-            last = jnp.max(node).astype(jnp.int32)
-            both = jnp.where(
-                is_grad,
-                jnp.broadcast_to(grad, (deep, tile_rows)),
-                jnp.broadcast_to(hess, (deep, tile_rows)),
-            )
-            node_wide = jnp.broadcast_to(node, (deep, tile_rows))
-            state.append((t, first, last, both, node_wide))
-        for u in range(UNROLL):
-            t, first, last, both, node_wide = state[u]
-            masked = node_block(u, 0, first, NODE_BLOCK, node_wide, both, True)
+            ranges.append((first, jnp.max(node).astype(jnp.int32)))
+        for u in range(per_vector):
+            node, node_wide, both = tile_sides(side_tile_ref, u)
+            masked = mask_nodes(ranges[u][0], NODE_BLOCK, node_wide, both)
             for q in range(quads):
                 for i in range(QUAD):
                     f = q * QUAD + i
-                    fine = jnp.broadcast_to(fine_ref[t, f : f + 1, :], (FINE, tile_rows))
+                    fine = jnp.broadcast_to(fine_ref[u, f : f + 1, :], (FINE, tile_rows))
                     stat_ref[u, q, i * FINE : (i + 1) * FINE, :] = jnp.where(
                         fine.astype(jnp.bfloat16) <= fine_index, one, zero
                     )
-                    coarse = jnp.broadcast_to(coarse_ref[t, f : f + 1, :], (deep, tile_rows))
-                    wide_ref[u, f] = coarse.astype(jnp.bfloat16)
-                add_product(u, q, first, masked)
-        for u in range(UNROLL):
-            t, first, last, both, node_wide = state[u]
+                    coarse = jnp.broadcast_to(coarse_ref[u, f : f + 1, :], (deep, tile_rows))
+                    wide_ref[u, f] = jnp.where(
+                        coarse.astype(jnp.bfloat16) == coarse_index, one, zero
+                    )
+                add_product(u, q, ranges[u][0], masked)
+        return ranges
+
+    def accumulate_rest(ranges, side_tile_ref):
+        for u in range(per_vector):
+            first, last = ranges[u]
 
             @pl.loop(first + NODE_BLOCK, last + 1)
             def _(n):
-                masked = node_block(u, 0, n, 1, node_wide, both, True)
+                node, node_wide, both = tile_sides(side_tile_ref, u)
+                masked = mask_nodes(n, 1, node_wide, both)
                 for q in range(quads):
                     add_product(u, q, n, masked)
 
+    even = (even_fine_ref, even_coarse_ref, even_side_ref)
+    odd = (odd_fine_ref, odd_coarse_ref, odd_side_ref)
+    prepare(0, *even)
+
+    @pl.loop(0, chunks // 2)
+    def _(pair):
+        ranges = accumulate(*even)
+        prepare(2 * pair + 1, *odd)
+        accumulate_rest(ranges, even_side_ref)
+        ranges = accumulate(*odd)
+        prepare(jnp.minimum(2 * pair + 2, chunks - 1), *even)
+        accumulate_rest(ranges, odd_side_ref)
+
     row = iota((COARSE, LANES), 0)
     last_lane = iota((COARSE, LANES), 1) | (FINE - 1)
 
     def left_sums(part):
-        ends = jnp.take_along_axis(part, last_lane, axis=1)
+        ends = look_up(part, last_lane)
         shift = 1
         while shift < COARSE:
             ends = ends + jnp.where(row >= shift, pltpu.roll(ends, shift, 0), 0.0)
             shift *= 2
         return part + jnp.where(row >= 1, pltpu.roll(ends, 1, 0), 0.0)
 
-    @pl.loop(0, NODES // 2)
-    def _(pair):
-        for k in range(2):
-            n = 2 * pair + k
-            sums = jnp.sum(total_ref[n], axis=1, keepdims=True)
-            grad_total = jnp.broadcast_to(sums[0:1], (COARSE, LANES))
-            hess_total = jnp.broadcast_to(sums[COARSE : COARSE + 1], (COARSE, LANES))
+    @pl.loop(0, NODES // 4)
+    def _(group):
+        for k in range(4):
+            n = 4 * group + k
+            grad_total = total_ref[n, :COARSE]
+            hess_total = total_ref[n, COARSE:]
             whole = jnp.square(grad_total) / (hess_total + PENALTY)
             for q in range(quads):
                 part = hist_ref[n, q]
@@ -301,7 +333,6 @@
     gathered = lax.all_to_all(sent, "row", 0, 0)
     edges = lax.dynamic_slice_in_dim(cut_points, lax.axis_index("row") * own, own, 0)
     tile_rows = PIECE * parts
-    tiles = rows // PIECE
     feature_gain, best = pl.pallas_call(
         gain_kernel,
         out_shape=(
@@ -312,11 +343,13 @@
         out_specs=(in_vmem, in_vmem),
         scratch_shapes=[
             pltpu.VMEM((parts, 24, LANES), jnp.float32),
-            pltpu.VMEM((tiles, own, tile_rows), jnp.float32),
-            pltpu.VMEM((tiles, own, tile_rows), jnp.float32),
-            pltpu.VMEM((tiles, 8, tile_rows), jnp.float32),
-            pltpu.VMEM((UNROLL, own // QUAD, QUAD * FINE, tile_rows), jnp.bfloat16),
-            pltpu.VMEM((UNROLL, own, 2 * COARSE, tile_rows), jnp.bfloat16),
+            pltpu.VMEM((32, own, LANES), jnp.float32),
+            *[
+                pltpu.VMEM((LANES // PIECE, height, tile_rows), jnp.float32)
+                for height in (own, own, 8, own, own, 8)
+            ],
+            pltpu.VMEM((LANES // PIECE, own // QUAD, QUAD * FINE, tile_rows), jnp.bfloat16),
+            pltpu.VMEM((LANES // PIECE, own, 2 * COARSE, tile_rows), jnp.bfloat16),
             pltpu.VMEM((NODES, own // QUAD, 2 * COARSE, LANES), jnp.float32),
             pltpu.VMEM((NODES, 2 * COARSE, LANES), jnp.float32),
             pltpu.VMEM((own // QUAD, NODES, LANES), jnp.float32),

time: 69.9 us -> 58.9 us (0.84)
  Pallas kernels: 29.7 us -> 18.7 us
    pallas_call x1, Pallas kernels: 27.9 us -> 16.9 us  [on_device(): pl.pallas_call(gain_kernel, out_shape=(jax.ShapeDtypeStruct((own, NODES),...]
where the time goes in v4:
time: 58.9 us; the launch traced here: 58.5 us
  Pallas kernels  18.7 us (32%)
  blocking collectives  17 us (29%)
  waiting for transfers between devices  11 us (19%)
  starting transfers between devices  7.34 us (12%)
  local copies, waits for them, and re-layouts  3.15 us (5%)
  other arithmetic  0.66 us (1%)
  between operations  0.66 us (1%)
    all_to_all x1, blocking collectives, on_device(): node_best = jnp.max(lax.all_to_all(best, ('row', 'feat'), 0, 0), axis=0)  17 us
    pallas_call x1, Pallas kernels, on_device(): pl.pallas_call(gain_kernel, out_shape=(jax.ShapeDtypeStruct((own, NODES),...  16.9 us
    all_to_all x1, waiting for transfers between devices, on_device(): gathered = lax.all_to_all(sent, 'row', 0, 0)  11 us
    all_to_all x1, starting transfers between devices, on_device(): gathered = lax.all_to_all(sent, 'row', 0, 0)  7.34 us
    unnamed x10, local copies, waits for them, and re-layouts  3.15 us
    pallas_call x1, Pallas kernels, on_device(): pl.pallas_call(sort_kernel, out_shape=jax.ShapeDtypeStruct((parts, length...  1.77 us
  transfers between devices with their start and end apart: 1, of which 1 were waited for; matrix products, arithmetic and copies ran while one was open for 0% of the time, Pallas kernels for 0%

profile of v4, /device:TPU:1, one launch (start us, length us, event | category | flops | bytes accessed | tf_op | source)
XLA Modules:
  0.0 58.5 jit_solution(14723438593135014127)
XLA Ops:
  0.6 0.0 copy-start
  0.6 0.0 copy-start.2
  0.7 0.7 %copy-done.2 = f32[1024]{0:T(1024)S(1)} copy-done((f32[1024]{0:T(1024)S(1)}, f32[1024]{0:T(1024)}, u32[]{:S(2)}) %copy-start.2) | copy-done | bytes 4120
  1.4 0.0 copy-start.1
  1.4 1.0 %copy-done.1 = bf16[1024,256]{1,0:T(8,128)(2,1)S(1)} copy-done((bf16[1024,256]{1,0:T(8,128)(2,1)S(1)}, bf16[1024,256]{1,0:T(8,128)(2,1)}, u32[]{:S(2)}) %copy-start.1) | copy-done | bytes 524312
  2.4 0.0 copy-start.3
  2.4 0.7 %copy-done.3 = f32[1024]{0:T(1024)S(1)} copy-done((f32[1024]{0:T(1024)S(1)}, f32[1024]{0:T(1024)}, u32[]{:S(2)}) %copy-start.3) | copy-done | bytes 4120
  3.1 0.0 copy-start.4
  3.1 0.7 %copy-done.4 = s32[1024]{0:T(1024)S(1)} copy-done((s32[1024]{0:T(1024)S(1)}, s32[1024]{0:T(1024)}, u32[]{:S(2)}) %copy-start.4) | copy-done | bytes 4120
  3.8 1.8 %sort_rows.1 = bf16[16,152,128]{2,1,0:T(8,128)(2,1)} custom-call(bf16[1024,256]{1,0:T(8,128)(2,1)S(1)} %copy-done.1, f32[1,1024]{1,0:T(1,128)S(1)} %bitcast.7, f32[1,1024]{1,0:T(1,128)S(1)} %bitcast.8, s32[1,1024]{1,0:T(1,128)S(1)} %bitcast.9), custom_call_target="tpu_custom_call" | custom-call | tf_op jit(solution)/shard_map/sort_rows/pallas_call | solution.py:325
  5.6 7.3 %all-to-all-start = ((bf16[16,152,128]{2,1,0:T(8,128)(2,1)}), bf16[16,152,128]{2,1,0:T(8,128)(2,1)S(1)}, u32[]{:S(2)}, u32[]{:S(2)}) async-start(bf16[16,152,128]{2,1,0:T(8,128)(2,1)} %sort_rows.1), calls=%async_computation | async-start | bytes 1245184 | tf_op jit(solution)/shard_map/all_to_all | solution.py:333
  12.9 0.0 copy-done
  12.9 11.0 %all-to-all-done.sent_ref = bf16[16,152,128]{2,1,0:T(8,128)(2,1)S(1)} async-done(((bf16[16,152,128]{2,1,0:T(8,128)(2,1)}), bf16[16,152,128]{2,1,0:T(8,128)(2,1)S(1)}, u32[]{:S(2)}, u32[]{:S(2)}) %all-to-all-start) | async-done | bytes 622624 | tf_op jit(solution)/shard_map/all_to_all | solution.py:333
  23.9 16.9 %split_gain.1 = (f32[16,32]{1,0:T(8,128)}, f32[128,32]{1,0:T(8,128)S(1)}) custom-call(bf16[16,152,128]{2,1,0:T(8,128)(2,1)S(1)} %all-to-all-done.sent_ref, f32[16,256]{1,0:T(8,128)S(1)} %constant_dynamic-slice_fusion.edge_ref), custom_call_target="tpu_custom_call" | custom-call | tf_op jit(solution)/shard_map/split_gain/pallas_call | solution.py:336
  40.9 17.0 %all_to_all.14 = f32[128,1,32]{2,1,0:T(1,128)S(1)} all-to-all(f32[128,1,32]{2,1,0:T(1,128)S(1)} %bitcast.6), channel_id=1, replica_groups=mesh['row'=16,'feat'=8] {'row','feat'}, dimensions={0} | all-to-all | bytes 32768 | tf_op jit(solution)/shard_map/all_to_all | solution.py:360
  57.9 0.7 %reduce_max.9 = f32[32]{0:T(128)} reduce(f32[128,1,32]{2,1,0:T(1,128)S(1)} %all_to_all.14, f32[]{:T(128)} %constant.13.clone.1), dimensions={0,1}, to_apply=%region_0.0 | reduce | flops 4064 | bytes 16516 | tf_op jit(solution)/shard_map/reduce_max | solution.py:360
  (1 shorter events, 0.0 us)
Async XLA Ops:
  0.6 12.3 %copy-start = (f32[256,256]{1,0:T(8,128)S(1)}, f32[256,256]{1,0:T(8,128)}, u32[]{:S(2)}) copy-start(f32[256,256]{1,0:T(8,128)} %param.6) | copy-start | bytes 786436
  0.6 0.7 %copy-start.2 = (f32[1024]{0:T(1024)S(1)}, f32[1024]{0:T(1024)}, u32[]{:S(2)}) copy-start(f32[1024]{0:T(1024)} %param.7) | copy-start | bytes 12292
  1.4 1.0 %copy-start.1 = (bf16[1024,256]{1,0:T(8,128)(2,1)S(1)}, bf16[1024,256]{1,0:T(8,128)(2,1)}, u32[]{:S(2)}) copy-start(bf16[1024,256]{1,0:T(8,128)(2,1)} %value_ref.1) | copy-start | bytes 1572868
  2.4 0.7 %copy-start.3 = (f32[1024]{0:T(1024)S(1)}, f32[1024]{0:T(1024)}, u32[]{:S(2)}) copy-start(f32[1024]{0:T(1024)} %param.8) | copy-start | bytes 12292
  3.1 0.7 %copy-start.4 = (s32[1024]{0:T(1024)S(1)}, s32[1024]{0:T(1024)}, u32[]{:S(2)}) copy-start(s32[1024]{0:T(1024)} %param.9) | copy-start | bytes 12292
  5.6 18.4 %all-to-all-start = ((bf16[16,152,128]{2,1,0:T(8,128)(2,1)}), bf16[16,152,128]{2,1,0:T(8,128)(2,1)S(1)}, u32[]{:S(2)}, u32[]{:S(2)}) async-start(bf16[16,152,128]{2,1,0:T(8,128)(2,1)} %sort_rows.1), calls=%async_computation | async-start | bytes 1245184 | tf_op jit(solution)/shard_map/all_to_all | solution.py:333

commit v5 on v4

--- a/solution.py
+++ b/solution.py
@@ -29,11 +29,21 @@
     return jnp.take_along_axis(table, index, axis=1, mode="promise_in_bounds")
 
 
-def sort_kernel(value_ref, grad_ref, hess_ref, node_ref, sent_ref):
+def sort_kernel(
+    value_in, grad_in, hess_in, node_in, sent_ref, value_ref, grad_ref, hess_ref, node_ref, arrived
+):
+    pairs = ((node_in, node_ref), (grad_in, grad_ref), (hess_in, hess_ref), (value_in, value_ref))
+    copies = [
+        pltpu.make_async_copy(source, target, arrived.at[k])
+        for k, (source, target) in enumerate(pairs)
+    ]
+    for copy in copies:
+        copy.start()
     rows, feats = value_ref.shape
     parts = sent_ref.shape[0]
     own = feats // parts
     chunks = rows // LANES
+    copies[0].wait()
     node = node_ref[...]
     member = (jnp.broadcast_to(node, (NODES, rows)) == iota((NODES, rows), 0)).astype(jnp.float32)
     earlier = (jnp.broadcast_to(node, (NODES, rows)) < iota((NODES, rows), 0)).astype(jnp.float32)
@@ -47,6 +57,8 @@
         offset = offset + jnp.sum(piece, axis=1, keepdims=True)
     rank = jnp.concatenate(ranks, axis=1).astype(jnp.int32)
 
+    for copy in copies[1:]:
+        copy.wait()
     side = jnp.concatenate(
         [grad_ref[...], hess_ref[...], node.astype(jnp.float32), jnp.zeros((13, rows), jnp.float32)],
         axis=0,
@@ -118,8 +130,11 @@
             ]
             wide = (NODES, 2 * LANES)
             member = jnp.where(
-                jnp.broadcast_to(node, wide) == iota(wide, 0).astype(jnp.float32), 1.0, 0.0
-            ).astype(jnp.bfloat16)
+                jnp.broadcast_to(node, wide).astype(jnp.bfloat16)
+                == iota(wide, 0).astype(jnp.float32).astype(jnp.bfloat16),
+                jnp.bfloat16(1),
+                jnp.bfloat16(0),
+            )
             both = jnp.concatenate(
                 [jnp.broadcast_to(grad, (8, 2 * LANES)), jnp.broadcast_to(hess, (8, 2 * LANES))], axis=0
             ).astype(jnp.bfloat16)
@@ -131,23 +146,23 @@
     edges = edge_ref[...]
     inner, leaf = search_tables(edges)
 
-    for j in range(32):
-        wide_edge_ref[j] = jnp.broadcast_to(edges[:, 8 * j : 8 * j + 1], (feats, LANES))
+    for j in range(8):
+        wide_edge_ref[j] = jnp.broadcast_to(edges[:, 32 * j : 32 * j + 1], (feats, LANES))
 
     def search(value):
         bits = []
-        for level in range(5):
-            choice = [wide_edge_ref[(2 * m + 1) << (4 - level)] for m in range(1 << level)]
+        for level in range(3):
+            choice = [wide_edge_ref[(2 * m + 1) << (2 - level)] for m in range(1 << level)]
             for bit in reversed(bits):
                 choice = [
                     jnp.where(bit, choice[2 * m + 1], choice[2 * m])
                     for m in range(len(choice) // 2)
                 ]
             bits.append(value >= choice[0])
-        place = jnp.where(bits[0], 48, 32)
-        for level in range(1, 5):
-            place = place + jnp.where(bits[level], 16 >> level, 0)
-        for level in range(5, 8):
+        place = jnp.where(bits[0], 12, 8)
+        for level in range(1, 3):
+            place = place + jnp.where(bits[level], 4 >> level, 0)
+        for level in range(3, 8):
             if level < 7:
                 edge = look_up(inner, place)
             else:
@@ -325,8 +340,15 @@
     sent = pl.pallas_call(
         sort_kernel,
         out_shape=jax.ShapeDtypeStruct((parts, length, LANES), jnp.bfloat16),
-        in_specs=[in_vmem] * 4,
+        in_specs=[pl.BlockSpec(memory_space=pltpu.MemorySpace.HBM)] * 4,
         out_specs=in_vmem,
+        scratch_shapes=[
+            pltpu.VMEM((rows, feats), jnp.bfloat16),
+            pltpu.VMEM((1, rows), jnp.float32),
+            pltpu.VMEM((1, rows), jnp.float32),
+            pltpu.VMEM((1, rows), jnp.int32),
+            pltpu.SemaphoreType.DMA((4,)),
+        ],
         name="sort_rows",
         compiler_params=pltpu.CompilerParams(vmem_limit_bytes=30 << 20),
     )(features, grad[None], hess[None], node_ids[None])
@@ -343,7 +365,7 @@
         out_specs=(in_vmem, in_vmem),
         scratch_shapes=[
             pltpu.VMEM((parts, 24, LANES), jnp.float32),
-            pltpu.VMEM((32, own, LANES), jnp.float32),
+            pltpu.VMEM((8, own, LANES), jnp.float32),
             *[
                 pltpu.VMEM((LANES // PIECE, height, tile_rows), jnp.float32)
                 for height in (own, own, 8, own, own, 8)

time: 58.9 us -> 57.2 us (0.971)
  Pallas kernels: 18.7 us -> 17 us
    pallas_call x1, Pallas kernels: 16.9 us -> 15.1 us  [on_device(): pl.pallas_call(gain_kernel, out_shape=(jax.ShapeDtypeStruct((own, NODES),...]
where the time goes in v5:
time: 57.2 us; the launch traced here: 56.8 us
  Pallas kernels  17 us (30%)
  blocking collectives  17 us (30%)
  waiting for transfers between devices  11 us (19%)
  starting transfers between devices  7.35 us (13%)
  local copies, waits for them, and re-layouts  3.15 us (6%)
  between operations  0.67 us (1%)
  other arithmetic  0.66 us (1%)
    all_to_all x1, blocking collectives, on_device(): node_best = jnp.max(lax.all_to_all(best, ('row', 'feat'), 0, 0), axis=0)  17 us
    pallas_call x1, Pallas kernels, on_device(): pl.pallas_call(gain_kernel, out_shape=(jax.ShapeDtypeStruct((own, NODES),...  15.1 us
    all_to_all x1, waiting for transfers between devices, on_device(): gathered = lax.all_to_all(sent, 'row', 0, 0)  11 us
    all_to_all x1, starting transfers between devices, on_device(): gathered = lax.all_to_all(sent, 'row', 0, 0)  7.35 us
    unnamed x10, local copies, waits for them, and re-layouts  3.15 us
    pallas_call x1, Pallas kernels, on_device(): pl.pallas_call(sort_kernel, out_shape=jax.ShapeDtypeStruct((parts, length...  1.89 us
  transfers between devices with their start and end apart: 1, of which 1 were waited for; matrix products, arithmetic and copies ran while one was open for 0% of the time, Pallas kernels for 0%

profile of v5, /device:TPU:1, one launch (start us, length us, event | category | flops | bytes accessed | tf_op | source)
XLA Modules:
  0.0 56.8 jit_solution(16669154093670440386)
XLA Ops:
  0.6 0.0 copy-start
  0.6 0.0 copy-start.2
  0.7 0.7 %copy-done.2 = f32[1024]{0:T(1024)S(1)} copy-done((f32[1024]{0:T(1024)S(1)}, f32[1024]{0:T(1024)}, u32[]{:S(2)}) %copy-start.2) | copy-done | bytes 4120
  1.4 0.0 copy-start.1
  1.4 1.0 %copy-done.1 = bf16[1024,256]{1,0:T(8,128)(2,1)S(1)} copy-done((bf16[1024,256]{1,0:T(8,128)(2,1)S(1)}, bf16[1024,256]{1,0:T(8,128)(2,1)}, u32[]{:S(2)}) %copy-start.1) | copy-done | bytes 524312
  2.4 0.0 copy-start.3
  2.4 0.7 %copy-done.3 = f32[1024]{0:T(1024)S(1)} copy-done((f32[1024]{0:T(1024)S(1)}, f32[1024]{0:T(1024)}, u32[]{:S(2)}) %copy-start.3) | copy-done | bytes 4120
  3.1 0.0 copy-start.4
  3.1 0.7 %copy-done.4 = s32[1024]{0:T(1024)S(1)} copy-done((s32[1024]{0:T(1024)S(1)}, s32[1024]{0:T(1024)}, u32[]{:S(2)}) %copy-start.4) | copy-done | bytes 4120
  3.8 1.9 %sort_rows.1 = bf16[16,152,128]{2,1,0:T(8,128)(2,1)} custom-call(bf16[1024,256]{1,0:T(8,128)(2,1)S(1)} %copy-done.1, f32[1,1024]{1,0:T(1,128)S(1)} %bitcast.7, f32[1,1024]{1,0:T(1,128)S(1)} %bitcast.8, s32[1,1024]{1,0:T(1,128)S(1)} %bitcast.9), custom_call_target="tpu_custom_call" | custom-call | tf_op jit(solution)/shard_map/sort_rows/pallas_call | solution.py:340
  5.7 7.4 %all-to-all-start = ((bf16[16,152,128]{2,1,0:T(8,128)(2,1)}), bf16[16,152,128]{2,1,0:T(8,128)(2,1)S(1)}, u32[]{:S(2)}, u32[]{:S(2)}) async-start(bf16[16,152,128]{2,1,0:T(8,128)(2,1)} %sort_rows.1), calls=%async_computation | async-start | bytes 1245184 | tf_op jit(solution)/shard_map/all_to_all | solution.py:355
  13.0 0.0 copy-done
  13.1 11.0 %all-to-all-done.sent_ref = bf16[16,152,128]{2,1,0:T(8,128)(2,1)S(1)} async-done(((bf16[16,152,128]{2,1,0:T(8,128)(2,1)}), bf16[16,152,128]{2,1,0:T(8,128)(2,1)S(1)}, u32[]{:S(2)}, u32[]{:S(2)}) %all-to-all-start) | async-done | bytes 622624 | tf_op jit(solution)/shard_map/all_to_all | solution.py:355
  24.1 15.1 %split_gain.1 = (f32[16,32]{1,0:T(8,128)}, f32[128,32]{1,0:T(8,128)S(1)}) custom-call(bf16[16,152,128]{2,1,0:T(8,128)(2,1)S(1)} %all-to-all-done.sent_ref, f32[16,256]{1,0:T(8,128)S(1)} %constant_dynamic-slice_fusion.edge_ref), custom_call_target="tpu_custom_call" | custom-call | tf_op jit(solution)/shard_map/split_gain/pallas_call | solution.py:358
  39.1 17.0 %all_to_all.14 = f32[128,1,32]{2,1,0:T(1,128)S(1)} all-to-all(f32[128,1,32]{2,1,0:T(1,128)S(1)} %bitcast.6), channel_id=1, replica_groups=mesh['row'=16,'feat'=8] {'row','feat'}, dimensions={0} | all-to-all | bytes 32768 | tf_op jit(solution)/shard_map/all_to_all | solution.py:382
  56.2 0.7 %reduce_max.9 = f32[32]{0:T(128)} reduce(f32[128,1,32]{2,1,0:T(1,128)S(1)} %all_to_all.14, f32[]{:T(128)} %constant.13.clone.1), dimensions={0,1}, to_apply=%region_0.0 | reduce | flops 4064 | bytes 16516 | tf_op jit(solution)/shard_map/reduce_max | solution.py:382
  (1 shorter events, 0.0 us)
Async XLA Ops:
  0.6 12.4 %copy-start = (f32[256,256]{1,0:T(8,128)S(1)}, f32[256,256]{1,0:T(8,128)}, u32[]{:S(2)}) copy-start(f32[256,256]{1,0:T(8,128)} %param.6) | copy-start | bytes 786436
  0.6 0.7 %copy-start.2 = (f32[1024]{0:T(1024)S(1)}, f32[1024]{0:T(1024)}, u32[]{:S(2)}) copy-start(f32[1024]{0:T(1024)} %param.7) | copy-start | bytes 12292
  1.4 1.0 %copy-start.1 = (bf16[1024,256]{1,0:T(8,128)(2,1)S(1)}, bf16[1024,256]{1,0:T(8,128)(2,1)}, u32[]{:S(2)}) copy-start(bf16[1024,256]{1,0:T(8,128)(2,1)} %value_in.1) | copy-start | bytes 1572868
  2.4 0.7 %copy-start.3 = (f32[1024]{0:T(1024)S(1)}, f32[1024]{0:T(1024)}, u32[]{:S(2)}) copy-start(f32[1024]{0:T(1024)} %param.8) | copy-start | bytes 12292
  3.1 0.7 %copy-start.4 = (s32[1024]{0:T(1024)S(1)}, s32[1024]{0:T(1024)}, u32[]{:S(2)}) copy-start(s32[1024]{0:T(1024)} %param.9) | copy-start | bytes 12292
  5.7 18.4 %all-to-all-start = ((bf16[16,152,128]{2,1,0:T(8,128)(2,1)}), bf16[16,152,128]{2,1,0:T(8,128)(2,1)S(1)}, u32[]{:S(2)}, u32[]{:S(2)}) async-start(bf16[16,152,128]{2,1,0:T(8,128)(2,1)} %sort_rows.1), calls=%async_computation | async-start | bytes 1245184 | tf_op jit(solution)/shard_map/all_to_all | solution.py:355
